TPU v7x, 256 devices: a whole 4x4x8 slice. The times are simulated.
256 devices in a mesh: height: 8 (over z_hi, core), plane: 32 (over z_lo, y, x).
Axes of the slice: x: 4, y: 4, z: 8 (z_hi: 4, z_lo: 2; z = z_hi * 2 + z_lo), core: 2. Of those that a mesh axis runs over, the one named last changes fastest.
Arguments:
- cotangent: float32 [128, 256, 128], P('height', 'plane'), may hold values from -36 to 36
- conductivity: float32 [16, 32, 16], P('height', 'plane'), may hold values from 0.2 to 5
- capacity: float32 [16, 32, 16], P('height', 'plane'), may hold values from 0.5 to 2
- sources: int32 [2, 128], replicated, may hold values from 0 to 8191
Outputs:
- adjoint_second: float32 [128, 256, 128], P('height', 'plane')
- adjoint_first: float32 [128, 256, 128], P('height', 'plane')
- source_grad: float32 [2, 128], replicated
Inputs may be any that keep to these rules, and one draw needn't show every extreme that they name: `sources`: element numbers; element (ez, ex, ey) has number (ez * 32 + ex) * 16 + ey, and a number may repeat.
All inputs are finite; a program needn't handle non-finite values.
Results may differ from a plain program's by a relative error of at most 0.0001.
Values sent between devices are 32-bit elements; how exact they have to be, the bound alone decides.
A program may use at most 64 MiB of HBM per device.

v0:
```python
import jax
import jax.numpy as jnp
import numpy as np
from jax import lax
from jax.sharding import Mesh
from jax.sharding import PartitionSpec as P

ITERS = 3
HEIGHT = ("height_0", "height_1")
PLANE = ("plane_0", "plane_1", "plane_2")
HEIGHT_PLANE = ("height_0", "height_1", "plane_0", "plane_1", "plane_2")


precise = lax.Precision.HIGHEST
INV_STEP = 20.0


def with_halo(block, sides, width):
    for axis, dim in sides:
        count = lax.axis_size(axis)
        forward = [(i, i + 1) for i in range(count - 1)]
        backward = [(target, source) for source, target in forward]
        low = lax.ppermute(
            lax.slice_in_dim(block, block.shape[dim] - width, None, axis=dim), axis, forward
        )
        high = lax.ppermute(lax.slice_in_dim(block, 0, width, axis=dim), axis, backward)
        block = jnp.concatenate([low, block, high], axis=dim)
    return block


def by_axis(value, axes):
    for axis in axes:
        value = lax.psum(value, axis)
    return value


def gll_tables():
    points = np.array(
        [
            -1.0,
            -0.8717401485096066,
            -0.5917001814331423,
            -0.2092992179024789,
            0.2092992179024789,
            0.5917001814331423,
            0.8717401485096066,
            1.0,
        ]
    )
    weights = np.array(
        [
            1.0 / 28.0,
            0.2107042271435061,
            0.3411226924835044,
            0.4124587946587038,
            0.4124587946587038,
            0.3411226924835044,
            0.2107042271435061,
            1.0 / 28.0,
        ]
    )
    product = np.array(
        [
            np.prod([points[column] - points[others] for others in range(8) if others != column])
            for column in range(8)
        ]
    )
    derivative = np.zeros((8, 8))
    for row_idx in range(8):
        for col_idx in range(8):
            if row_idx != col_idx:
                derivative[row_idx, col_idx] = product[row_idx] / (
                    product[col_idx] * (points[row_idx] - points[col_idx])
                )
        derivative[row_idx, row_idx] = -np.sum(derivative[row_idx])
    stiff_diag = np.sum(derivative**2 * weights[:, None], axis=0)
    return (derivative, weights, stiff_diag)


def pair_sum(values, dim_index):
    shape = values.shape
    count = shape[dim_index] // 8
    split = values.reshape(shape[:dim_index] + (count, 8) + shape[dim_index + 1 :])
    slot_axis = dim_index + 1
    slot_first = lax.slice_in_dim(split, 0, 1, axis=slot_axis)
    slot_last = lax.slice_in_dim(split, 7, 8, axis=slot_axis)
    middle = lax.slice_in_dim(split, 1, 7, axis=slot_axis)
    joined = lax.slice_in_dim(slot_last, 0, count - 1, axis=dim_index) + lax.slice_in_dim(
        slot_first, 1, count, axis=dim_index
    )
    new_last = jnp.concatenate(
        [joined, lax.slice_in_dim(slot_last, count - 1, count, axis=dim_index)], axis=dim_index
    )
    new_first = jnp.concatenate(
        [lax.slice_in_dim(slot_first, 0, 1, axis=dim_index), joined], axis=dim_index
    )
    rebuilt = jnp.concatenate([new_first, middle, new_last], axis=slot_axis)
    return rebuilt.reshape(shape)


def add_edges(values, lower, upper, dim_index):
    extent = values.shape[dim_index]
    first = lax.slice_in_dim(values, 0, 1, axis=dim_index) + jnp.expand_dims(lower, dim_index)
    inside = lax.slice_in_dim(values, 1, extent - 1, axis=dim_index)
    last = lax.slice_in_dim(values, extent - 1, extent, axis=dim_index) + jnp.expand_dims(
        upper, dim_index
    )
    return jnp.concatenate([first, inside, last], axis=dim_index)


def multiplicity(local_count, offset, extent):
    position = offset + jnp.arange(local_count, dtype=jnp.int32)
    ending = ((position % 8 == 7) & (position < extent - 1)).astype(jnp.float32)
    opening = ((position % 8 == 0) & (position > 0)).astype(jnp.float32)
    return 1.0 + ending + opening


def per_device(cotangent, conductivity, capacity, sources):
    derivative, weights, stiff_diag = gll_tables()
    depth_nodes, width_nodes, span_nodes = cotangent.shape
    elem_depth, elem_width, elem_span = (depth_nodes // 8, width_nodes // 8, span_nodes // 8)
    diff = jnp.asarray(derivative, jnp.float32)
    weight_depth = jnp.asarray(np.tile(weights, elem_depth), jnp.float32)
    weight_width = jnp.asarray(np.tile(weights, elem_width), jnp.float32)
    weight_span = jnp.asarray(np.tile(weights, elem_span), jnp.float32)
    stiff_depth = jnp.asarray(np.tile(stiff_diag, elem_depth), jnp.float32)
    stiff_width = jnp.asarray(np.tile(stiff_diag, elem_width), jnp.float32)
    stiff_span = jnp.asarray(np.tile(stiff_diag, elem_span), jnp.float32)
    kappa_nodes = jnp.repeat(jnp.repeat(jnp.repeat(conductivity, 8, axis=0), 8, axis=1), 8, axis=2)
    cap_nodes = jnp.repeat(jnp.repeat(jnp.repeat(capacity, 8, axis=0), 8, axis=1), 8, axis=2)
    omega_nodes = (
        weight_depth[:, None, None] * weight_width[None, :, None] * weight_span[None, None, :]
    )
    mass_local = INV_STEP * cap_nodes * omega_nodes
    kappa_weight = kappa_nodes * omega_nodes
    diag_local = mass_local + kappa_nodes * (
        stiff_depth[:, None, None] * weight_width[None, :, None] * weight_span[None, None, :]
        + weight_depth[:, None, None] * stiff_width[None, :, None] * weight_span[None, None, :]
        + weight_depth[:, None, None] * weight_width[None, :, None] * stiff_span[None, None, :]
    )
    height_pos = lax.axis_index(HEIGHT)
    plane_pos = lax.axis_index(PLANE)
    copies_depth = multiplicity(
        depth_nodes, height_pos * depth_nodes, depth_nodes * lax.axis_size(HEIGHT)
    )
    copies_width = multiplicity(
        width_nodes, plane_pos * width_nodes, width_nodes * lax.axis_size(PLANE)
    )
    copies_span = multiplicity(span_nodes, 0, span_nodes)
    share_weight = 1.0 / (
        copies_depth[:, None, None] * copies_width[None, :, None] * copies_span[None, None, :]
    )
    shape_depth = (elem_depth, 8, width_nodes, span_nodes)
    shape_width = (depth_nodes, elem_width, 8, span_nodes)
    shape_span = (depth_nodes, width_nodes, elem_span, 8)
    full_shape = cotangent.shape

    def stiffness(values):
        grad_depth = jnp.einsum(
            "ab,ebxy->eaxy", diff, values.reshape(shape_depth), precision=precise
        ).reshape(full_shape)
        grad_width = jnp.einsum(
            "ab,zeby->zeay", diff, values.reshape(shape_width), precision=precise
        ).reshape(full_shape)
        grad_span = jnp.einsum(
            "ab,zxeb->zxea", diff, values.reshape(shape_span), precision=precise
        ).reshape(full_shape)
        back_depth = jnp.einsum(
            "ab,eaxy->ebxy",
            diff,
            (kappa_weight * grad_depth).reshape(shape_depth),
            precision=precise,
        ).reshape(full_shape)
        back_width = jnp.einsum(
            "ab,zeay->zeby",
            diff,
            (kappa_weight * grad_width).reshape(shape_width),
            precision=precise,
        ).reshape(full_shape)
        back_span = jnp.einsum(
            "ab,zxea->zxeb", diff, (kappa_weight * grad_span).reshape(shape_span), precision=precise
        ).reshape(full_shape)
        return mass_local * values + (back_depth + back_width + back_span)

    def assemble(contrib):
        summed = pair_sum(contrib, 1)
        face_pair = jnp.stack([summed[:, 0], summed[:, -1]])
        received = with_halo(face_pair, ((PLANE, 0),), 1)
        summed = add_edges(summed, received[0], received[3], 1)
        summed = pair_sum(summed, 2)
        summed = pair_sum(summed, 0)
        face_pair = jnp.stack([summed[0], summed[-1]])
        received = with_halo(face_pair, ((HEIGHT, 0),), 1)
        summed = add_edges(summed, received[0], received[3], 0)
        return summed

    diag_total = assemble(diag_local)

    def inner_sum(left_values, right_values):
        return jnp.sum(left_values * right_values * share_weight)

    def paired_sums(residual, precond, applied):
        return (
            by_axis(inner_sum(residual, precond), HEIGHT_PLANE),
            by_axis(inner_sum(precond, applied), HEIGHT_PLANE),
        )

    def adjoint_solve(source_term):
        iterate = jnp.zeros_like(source_term)
        residual = source_term
        precond = residual / diag_total
        applied = assemble(stiffness(precond))
        rho_now, curvature_now = paired_sums(residual, precond, applied)
        step_len = rho_now / curvature_now
        direction, applied_dir = (precond, applied)
        for sweep_idx in range(ITERS):
            iterate = iterate + step_len * direction
            residual = residual - step_len * applied_dir
            if sweep_idx + 1 < ITERS:
                precond = residual / diag_total
                applied = assemble(stiffness(precond))
                rho_next, curvature_now = paired_sums(residual, precond, applied)
                beta_now = rho_next / rho_now
                step_len = rho_next / (curvature_now - beta_now * rho_next / step_len)
                direction = precond + beta_now * direction
                applied_dir = applied + beta_now * applied_dir
                rho_now = rho_next
        return iterate

    adjoint_second = adjoint_solve(assemble(mass_local * cotangent))
    adjoint_first = adjoint_solve(assemble(mass_local * adjoint_second))

    def element_sums(values):
        return (
            (mass_local * values)
            .reshape(elem_depth, 8, elem_width, 8, elem_span, 8)
            .sum(axis=(1, 3, 5))
            .reshape(-1)
        )

    depth_ids = height_pos * elem_depth + jnp.arange(elem_depth, dtype=jnp.int32)
    width_ids = plane_pos * elem_width + jnp.arange(elem_width, dtype=jnp.int32)
    span_ids = jnp.arange(elem_span, dtype=jnp.int32)
    global_ids = (
        (depth_ids[:, None, None] * (elem_width * lax.axis_size(PLANE)) + width_ids[None, :, None])
        * elem_span
        + span_ids[None, None, :]
    ).reshape(-1)
    matches = (sources[:, :, None] == global_ids[None, None, :]).astype(jnp.float32)
    stacked = jnp.stack([element_sums(adjoint_first), element_sums(adjoint_second)])
    local_grad = jnp.sum(matches * stacked[:, None, :], axis=2) / (8.0 * INV_STEP)
    source_grad = by_axis(local_grad, HEIGHT_PLANE)
    return (adjoint_second, adjoint_first, source_grad)


def solution(mesh):
    torus = Mesh(
        mesh.devices.reshape(4, 2, 2, 4, 4),
        ("height_0", "height_1", "plane_0", "plane_1", "plane_2"),
    )
    in_specs = (P(HEIGHT, PLANE, None), P(HEIGHT, PLANE, None), P(HEIGHT, PLANE, None), P())
    out_specs = (P(HEIGHT, PLANE, None), P(HEIGHT, PLANE, None), P())
    return jax.shard_map(
        per_device, mesh=torus, in_specs=in_specs, out_specs=out_specs, check_vma=False
    )
```

profile of v0, /device:TPU:32, one launch (start us, length us, event | category | flops | bytes accessed | tf_op | source)
XLA Modules:
  0.0 619.1 jit_solution(5924039357253997425)
XLA Ops:
  3.8 6.7 %collective-permute-start.5 = (f32[1,16,128]{2,1,0:T(8,128)S(1)}, f32[1,16,128]{2,1,0:T(8,128)S(1)}, u32[]{:S(2)}, u32[]{:S(2)}) collective-permute-start(f32[1,16,128]{2,1,0:T(8,128)S(1)} %bitcast.647), channel_id=1, source_target_pairs={{1,0},{2,1},{3,2},{4,3},{5,4},{6,5},{7,6},{8,7},{9,8},{10,9},{11,1... | collective-permute-start | bytes 24584 | tf_op jit(solution)/shard_map/ppermute | solution.py:26
  45.8 6.5 %collective-permute-start.2 = (f32[1,8,128]{2,1,0:T(8,128)S(1)}, f32[1,8,128]{2,1,0:T(8,128)S(1)}, u32[]{:S(2)}, u32[]{:S(2)}) collective-permute-start(f32[1,8,128]{2,1,0:T(8,128)S(1)} %get-tuple-element.211), channel_id=1, source_target_pairs={{0,32},{32,64},{64,96},{96,128},{128,160},{160,192},{192,224},{1,3... | collective-permute-start | bytes 12296 | tf_op jit(solution)/shard_map/ppermute | solution.py:23
  70.9 7.3 %collective-permute-done.8 = f32[1,16,128]{2,1,0:T(8,128)S(1)} collective-permute-done((f32[1,16,128]{2,1,0:T(8,128)S(1)}, f32[1,16,128]{2,1,0:T(8,128)S(1)}, u32[]{:S(2)}, u32[]{:S(2)}) %collective-permute-start.8) | collective-permute-done | bytes 8224 | tf_op jit(solution)/shard_map/ppermute | solution.py:23
  98.0 14.5 %all-reduce.17 = (f32[]{:T(128)}, f32[]{:T(128)}) all-reduce(f32[]{:T(128)} %get-tuple-element.14, f32[]{:T(128)} %get-tuple-element.13), channel_id=1, replica_groups=mesh['height_0'=4,'height_1'=2,'plane_0'=2,'plane_1'=4,'plane_2'=4] {'he..., use_global_device_ids=true, to_apply=%region_1.2 | all-reduce | flops 2 | bytes 16 | tf_op jit(solution)/shard_map/psum | solution.py:33
  117.5 5.6 all-reduce.23
  123.1 8.4 %all-reduce.11 = (f32[]{:T(128)}, f32[]{:T(128)}) all-reduce(f32[]{:T(128)} %get-tuple-element.61, f32[]{:T(128)} %get-tuple-element.62), channel_id=1, replica_groups=mesh['height_0'=4,'height_1'=2,'plane_0'=2,'plane_1'=4,'plane_2'=4] {'pl..., use_global_device_ids=true, to_apply=%region_4.5 | all-reduce | flops 2 | bytes 16 | tf_op jit(solution)/shard_map/psum | solution.py:33
  131.5 9.3 %all-reduce.5 = (f32[]{:T(128)}, f32[]{:T(128)}) all-reduce(f32[]{:T(128)} %get-tuple-element.37, f32[]{:T(128)} %get-tuple-element.38), channel_id=1, replica_groups=mesh['height_0'=4,'height_1'=2,'plane_0'=2,'plane_1'=4,'plane_2'=4] {'pl..., use_global_device_ids=true, to_apply=%region_5.6 | all-reduce | flops 2 | bytes 16 | tf_op jit(solution)/shard_map/psum | solution.py:33
  155.7 6.7 %collective-permute-done.12 = f32[1,16,128]{2,1,0:T(8,128)S(1)} collective-permute-done((f32[1,16,128]{2,1,0:T(8,128)S(1)}, f32[1,16,128]{2,1,0:T(8,128)S(1)}, u32[]{:S(2)}, u32[]{:S(2)}) %collective-permute-start.12) | collective-permute-done | bytes 8224 | tf_op jit(solution)/shard_map/ppermute | solution.py:23
  178.2 13.6 %all-reduce.16 = (f32[]{:T(128)}, f32[]{:T(128)}) all-reduce(f32[]{:T(128)} %get-tuple-element.12, f32[]{:T(128)} %get-tuple-element.11), channel_id=1, replica_groups=mesh['height_0'=4,'height_1'=2,'plane_0'=2,'plane_1'=4,'plane_2'=4] {'he..., use_global_device_ids=true, to_apply=%region_13.14 | all-reduce | flops 2 | bytes 16 | tf_op jit(solution)/shard_map/psum | solution.py:33
  201.4 8.4 %all-reduce.10 = (f32[]{:T(128)}, f32[]{:T(128)}) all-reduce(f32[]{:T(128)} %get-tuple-element.59, f32[]{:T(128)} %get-tuple-element.60), channel_id=1, replica_groups=mesh['height_0'=4,'height_1'=2,'plane_0'=2,'plane_1'=4,'plane_2'=4] {'pl..., use_global_device_ids=true, to_apply=%region_16.17 | all-reduce | flops 2 | bytes 16 | tf_op jit(solution)/shard_map/psum | solution.py:33
  209.8 9.9 %all-reduce.4 = (f32[]{:T(128)}, f32[]{:T(128)}) all-reduce(f32[]{:T(128)} %get-tuple-element.35, f32[]{:T(128)} %get-tuple-element.36), channel_id=1, replica_groups=mesh['height_0'=4,'height_1'=2,'plane_0'=2,'plane_1'=4,'plane_2'=4] {'pl..., use_global_device_ids=true, to_apply=%region_17.18 | all-reduce | flops 2 | bytes 16 | tf_op jit(solution)/shard_map/psum | solution.py:33
  238.0 6.9 %collective-permute-done.16 = f32[1,16,128]{2,1,0:T(8,128)S(1)} collective-permute-done((f32[1,16,128]{2,1,0:T(8,128)S(1)}, f32[1,16,128]{2,1,0:T(8,128)S(1)}, u32[]{:S(2)}, u32[]{:S(2)}) %collective-permute-start.16) | collective-permute-done | bytes 8224 | tf_op jit(solution)/shard_map/ppermute | solution.py:23
  260.7 13.7 %all-reduce.15 = (f32[]{:T(128)}, f32[]{:T(128)}) all-reduce(f32[]{:T(128)} %get-tuple-element.10, f32[]{:T(128)} %get-tuple-element.9), channel_id=1, replica_groups=mesh['height_0'=4,'height_1'=2,'plane_0'=2,'plane_1'=4,'plane_2'=4] {'he..., use_global_device_ids=true, to_apply=%region_25.26 | all-reduce | flops 2 | bytes 16 | tf_op jit(solution)/shard_map/psum | solution.py:33
  283.9 8.3 %all-reduce.9 = (f32[]{:T(128)}, f32[]{:T(128)}) all-reduce(f32[]{:T(128)} %get-tuple-element.57, f32[]{:T(128)} %get-tuple-element.58), channel_id=1, replica_groups=mesh['height_0'=4,'height_1'=2,'plane_0'=2,'plane_1'=4,'plane_2'=4] {'pl..., use_global_device_ids=true, to_apply=%region_28.29 | all-reduce | flops 2 | bytes 16 | tf_op jit(solution)/shard_map/psum | solution.py:33
  292.2 9.3 %all-reduce.3 = (f32[]{:T(128)}, f32[]{:T(128)}) all-reduce(f32[]{:T(128)} %get-tuple-element.33, f32[]{:T(128)} %get-tuple-element.34), channel_id=1, replica_groups=mesh['height_0'=4,'height_1'=2,'plane_0'=2,'plane_1'=4,'plane_2'=4] {'pl..., use_global_device_ids=true, to_apply=%region_29.30 | all-reduce | flops 2 | bytes 16 | tf_op jit(solution)/shard_map/psum | solution.py:33
  313.1 7.6 %collective-permute-done.20 = f32[1,16,128]{2,1,0:T(8,128)S(1)} collective-permute-done((f32[1,16,128]{2,1,0:T(8,128)S(1)}, f32[1,16,128]{2,1,0:T(8,128)S(1)}, u32[]{:S(2)}, u32[]{:S(2)}) %collective-permute-start.20) | collective-permute-done | bytes 8224 | tf_op jit(solution)/shard_map/ppermute | solution.py:23
  348.2 7.6 %collective-permute-done.24 = f32[1,16,128]{2,1,0:T(8,128)S(1)} collective-permute-done((f32[1,16,128]{2,1,0:T(8,128)S(1)}, f32[1,16,128]{2,1,0:T(8,128)S(1)}, u32[]{:S(2)}, u32[]{:S(2)}) %collective-permute-start.24) | collective-permute-done | bytes 8224 | tf_op jit(solution)/shard_map/ppermute | solution.py:23
  373.8 13.8 %all-reduce.14 = (f32[]{:T(128)}, f32[]{:T(128)}) all-reduce(f32[]{:T(128)} %get-tuple-element.8, f32[]{:T(128)} %get-tuple-element.7), channel_id=1, replica_groups=mesh['height_0'=4,'height_1'=2,'plane_0'=2,'plane_1'=4,'plane_2'=4] {'he..., use_global_device_ids=true, to_apply=%region_37.38 | all-reduce | flops 2 | bytes 16 | tf_op jit(solution)/shard_map/psum | solution.py:33
  392.6 5.6 all-reduce.20
  398.2 8.4 %all-reduce.8 = (f32[]{:T(128)}, f32[]{:T(128)}) all-reduce(f32[]{:T(128)} %get-tuple-element.55, f32[]{:T(128)} %get-tuple-element.56), channel_id=1, replica_groups=mesh['height_0'=4,'height_1'=2,'plane_0'=2,'plane_1'=4,'plane_2'=4] {'pl..., use_global_device_ids=true, to_apply=%region_40.41 | all-reduce | flops 2 | bytes 16 | tf_op jit(solution)/shard_map/psum | solution.py:33
  406.7 8.4 %all-reduce.2 = (f32[]{:T(128)}, f32[]{:T(128)}) all-reduce(f32[]{:T(128)} %get-tuple-element.31, f32[]{:T(128)} %get-tuple-element.32), channel_id=1, replica_groups=mesh['height_0'=4,'height_1'=2,'plane_0'=2,'plane_1'=4,'plane_2'=4] {'pl..., use_global_device_ids=true, to_apply=%region_41.42 | all-reduce | flops 2 | bytes 16 | tf_op jit(solution)/shard_map/psum | solution.py:33
  431.5 5.7 collective-permute-done.28
  453.1 13.6 %all-reduce.13 = (f32[]{:T(128)}, f32[]{:T(128)}) all-reduce(f32[]{:T(128)} %get-tuple-element.6, f32[]{:T(128)} %get-tuple-element.5), channel_id=1, replica_groups=mesh['height_0'=4,'height_1'=2,'plane_0'=2,'plane_1'=4,'plane_2'=4] {'he..., use_global_device_ids=true, to_apply=%region_49.50 | all-reduce | flops 2 | bytes 16 | tf_op jit(solution)/shard_map/psum | solution.py:33
  476.2 8.4 %all-reduce.7 = (f32[]{:T(128)}, f32[]{:T(128)}) all-reduce(f32[]{:T(128)} %get-tuple-element.53, f32[]{:T(128)} %get-tuple-element.54), channel_id=1, replica_groups=mesh['height_0'=4,'height_1'=2,'plane_0'=2,'plane_1'=4,'plane_2'=4] {'pl..., use_global_device_ids=true, to_apply=%region_52.53 | all-reduce | flops 2 | bytes 16 | tf_op jit(solution)/shard_map/psum | solution.py:33
  484.6 9.5 %all-reduce.1 = (f32[]{:T(128)}, f32[]{:T(128)}) all-reduce(f32[]{:T(128)} %get-tuple-element.29, f32[]{:T(128)} %get-tuple-element.30), channel_id=1, replica_groups=mesh['height_0'=4,'height_1'=2,'plane_0'=2,'plane_1'=4,'plane_2'=4] {'pl..., use_global_device_ids=true, to_apply=%region_53.54 | all-reduce | flops 2 | bytes 16 | tf_op jit(solution)/shard_map/psum | solution.py:33
  512.2 6.6 %collective-permute-done.32 = f32[1,16,128]{2,1,0:T(8,128)S(1)} collective-permute-done((f32[1,16,128]{2,1,0:T(8,128)S(1)}, f32[1,16,128]{2,1,0:T(8,128)S(1)}, u32[]{:S(2)}, u32[]{:S(2)}) %collective-permute-start.32) | collective-permute-done | bytes 8224 | tf_op jit(solution)/shard_map/ppermute | solution.py:23
  534.5 13.6 %all-reduce.12 = (f32[]{:T(128)}, f32[]{:T(128)}) all-reduce(f32[]{:T(128)} %get-tuple-element.4, f32[]{:T(128)} %get-tuple-element.3), channel_id=1, replica_groups=mesh['height_0'=4,'height_1'=2,'plane_0'=2,'plane_1'=4,'plane_2'=4] {'he..., use_global_device_ids=true, to_apply=%region_61.62 | all-reduce | flops 2 | bytes 16 | tf_op jit(solution)/shard_map/psum | solution.py:33
  557.5 8.3 %all-reduce.6 = (f32[]{:T(128)}, f32[]{:T(128)}) all-reduce(f32[]{:T(128)} %get-tuple-element.51, f32[]{:T(128)} %get-tuple-element.52), channel_id=1, replica_groups=mesh['height_0'=4,'height_1'=2,'plane_0'=2,'plane_1'=4,'plane_2'=4] {'pl..., use_global_device_ids=true, to_apply=%region_64.65 | all-reduce | flops 2 | bytes 16 | tf_op jit(solution)/shard_map/psum | solution.py:33
  565.9 9.2 %all-reduce = (f32[]{:T(128)}, f32[]{:T(128)}) all-reduce(f32[]{:T(128)} %get-tuple-element.27, f32[]{:T(128)} %get-tuple-element.28), channel_id=1, replica_groups=mesh['height_0'=4,'height_1'=2,'plane_0'=2,'plane_1'=4,'plane_2'=4] {'pl..., use_global_device_ids=true, to_apply=%region_65.66 | all-reduce | flops 2 | bytes 16 | tf_op jit(solution)/shard_map/psum | solution.py:33
  580.9 10.9 %psum.515 = f32[2,128]{1,0:T(2,128)S(1)} all-reduce(f32[2,128]{1,0:T(2,128)S(1)} %broadcast_multiply_fusion.5), channel_id=1, replica_groups=mesh['height_0'=4,'height_1'=2,'plane_0'=2,'plane_1'=4,'plane_2'=4] {'he..., use_global_device_ids=true, to_apply=%region_79.80 | all-reduce | flops 256 | bytes 2048 | tf_op jit(solution)/shard_map/psum | solution.py:33
  599.1 8.8 %psum.518 = f32[2,128]{1,0:T(2,128)S(1)} all-reduce(f32[2,128]{1,0:T(2,128)S(1)} %psum.517), channel_id=1, replica_groups=mesh['height_0'=4,'height_1'=2,'plane_0'=2,'plane_1'=4,'plane_2'=4] {'pl..., use_global_device_ids=true, to_apply=%region_82.83 | all-reduce | flops 256 | bytes 2048 | tf_op jit(solution)/shard_map/psum | solution.py:33
  608.0 10.3 %psum.519 = f32[2,128]{1,0:T(2,128)} all-reduce(f32[2,128]{1,0:T(2,128)S(1)} %psum.518), channel_id=1, replica_groups=mesh['height_0'=4,'height_1'=2,'plane_0'=2,'plane_1'=4,'plane_2'=4] {'pl..., use_global_device_ids=true, to_apply=%region_83.84 | all-reduce | flops 256 | bytes 2048 | tf_op jit(solution)/shard_map/psum | solution.py:33
  (773 shorter events, 303.2 us)
Async XLA Ops:
  3.8 10.8 %collective-permute-start.5 = (f32[1,16,128]{2,1,0:T(8,128)S(1)}, f32[1,16,128]{2,1,0:T(8,128)S(1)}, u32[]{:S(2)}, u32[]{:S(2)}) collective-permute-start(f32[1,16,128]{2,1,0:T(8,128)S(1)} %bitcast.647), channel_id=1, source_target_pairs={{1,0},{2,1},{3,2},{4,3},{5,4},{6,5},{7,6},{8,7},{9,8},{10,9},{11,1... | collective-permute-start | bytes 24584 | tf_op jit(solution)/shard_map/ppermute | solution.py:26
  10.4 7.3 %collective-permute-start.1 = (f32[1,16,128]{2,1,0:T(8,128)S(1)}, f32[1,16,128]{2,1,0:T(8,128)S(1)}, u32[]{:S(2)}, u32[]{:S(2)}) collective-permute-start(f32[1,16,128]{2,1,0:T(8,128)S(1)} %bitcast.645), channel_id=1, source_target_pairs={{1,0},{2,1},{3,2},{4,3},{5,4},{6,5},{7,6},{8,7},{9,8},{10,9},{11,1... | collective-permute-start | bytes 24584 | tf_op jit(solution)/shard_map/ppermute | solution.py:26
  14.6 9.8 %collective-permute-start.4 = (f32[1,16,128]{2,1,0:T(8,128)S(1)}, f32[1,16,128]{2,1,0:T(8,128)S(1)}, u32[]{:S(2)}, u32[]{:S(2)}) collective-permute-start(f32[1,16,128]{2,1,0:T(8,128)S(1)} %bitcast.667), channel_id=1, source_target_pairs={{0,1},{1,2},{2,3},{3,4},{4,5},{5,6},{6,7},{7,8},{8,9},{9,10},{10,1... | collective-permute-start | bytes 24584 | tf_op jit(solution)/shard_map/ppermute | solution.py:23
  17.7 13.2 %collective-permute-start = (f32[1,16,128]{2,1,0:T(8,128)S(1)}, f32[1,16,128]{2,1,0:T(8,128)S(1)}, u32[]{:S(2)}, u32[]{:S(2)}) collective-permute-start(f32[1,16,128]{2,1,0:T(8,128)S(1)} %bitcast.666), channel_id=1, source_target_pairs={{0,1},{1,2},{2,3},{3,4},{4,5},{5,6},{6,7},{7,8},{8,9},{9,10},{10,1... | collective-permute-start | bytes 24584 | tf_op jit(solution)/shard_map/ppermute | solution.py:23
  41.0 14.3 %collective-permute-start.6 = (f32[1,8,128]{2,1,0:T(8,128)S(1)}, f32[1,8,128]{2,1,0:T(8,128)S(1)}, u32[]{:S(2)}, u32[]{:S(2)}) collective-permute-start(f32[1,8,128]{2,1,0:T(8,128)S(1)} %get-tuple-element.205), channel_id=1, source_target_pairs={{0,32},{32,64},{64,96},{96,128},{128,160},{160,192},{192,224},{1,3... | collective-permute-start | bytes 12296 | tf_op jit(solution)/shard_map/ppermute | solution.py:23
  42.4 12.9 %collective-permute-start.7 = (f32[1,8,128]{2,1,0:T(8,128)S(1)}, f32[1,8,128]{2,1,0:T(8,128)S(1)}, u32[]{:S(2)}, u32[]{:S(2)}) collective-permute-start(f32[1,8,128]{2,1,0:T(8,128)S(1)} %get-tuple-element.206), channel_id=1, source_target_pairs={{32,0},{64,32},{96,64},{128,96},{160,128},{192,160},{224,192},{33,... | collective-permute-start | bytes 12296 | tf_op jit(solution)/shard_map/ppermute | solution.py:26
  45.8 9.7 %collective-permute-start.2 = (f32[1,8,128]{2,1,0:T(8,128)S(1)}, f32[1,8,128]{2,1,0:T(8,128)S(1)}, u32[]{:S(2)}, u32[]{:S(2)}) collective-permute-start(f32[1,8,128]{2,1,0:T(8,128)S(1)} %get-tuple-element.211), channel_id=1, source_target_pairs={{0,32},{32,64},{64,96},{96,128},{128,160},{160,192},{192,224},{1,3... | collective-permute-start | bytes 12296 | tf_op jit(solution)/shard_map/ppermute | solution.py:23
  52.4 5.2 collective-permute-start.3
  62.8 5.5 collective-permute-start.9
  68.4 9.8 %collective-permute-start.8 = (f32[1,16,128]{2,1,0:T(8,128)S(1)}, f32[1,16,128]{2,1,0:T(8,128)S(1)}, u32[]{:S(2)}, u32[]{:S(2)}) collective-permute-start(f32[1,16,128]{2,1,0:T(8,128)S(1)} %bitcast.672), channel_id=1, source_target_pairs={{0,1},{1,2},{2,3},{3,4},{4,5},{5,6},{6,7},{7,8},{8,9},{9,10},{10,1... | collective-permute-start | bytes 24584 | tf_op jit(solution)/shard_map/ppermute | solution.py:23
  86.7 5.0 collective-permute-start.10
  89.6 7.4 %collective-permute-start.11 = (f32[1,8,128]{2,1,0:T(8,128)S(1)}, f32[1,8,128]{2,1,0:T(8,128)S(1)}, u32[]{:S(2)}, u32[]{:S(2)}) collective-permute-start(f32[1,8,128]{2,1,0:T(8,128)S(1)} %get-tuple-element.193), channel_id=1, source_target_pairs={{32,0},{64,32},{96,64},{128,96},{160,128},{192,160},{224,192},{33,... | collective-permute-start | bytes 12296 | tf_op jit(solution)/shard_map/ppermute | solution.py:26
  146.8 5.5 collective-permute-start.13
  152.4 10.0 %collective-permute-start.12 = (f32[1,16,128]{2,1,0:T(8,128)S(1)}, f32[1,16,128]{2,1,0:T(8,128)S(1)}, u32[]{:S(2)}, u32[]{:S(2)}) collective-permute-start(f32[1,16,128]{2,1,0:T(8,128)S(1)} %bitcast.674), channel_id=1, source_target_pairs={{0,1},{1,2},{2,3},{3,4},{4,5},{5,6},{6,7},{7,8},{8,9},{9,10},{10,1... | collective-permute-start | bytes 24584 | tf_op jit(solution)/shard_map/ppermute | solution.py:23
  172.3 4.4 collective-permute-start.15
  229.6 5.5 collective-permute-start.17
  235.1 9.8 %collective-permute-start.16 = (f32[1,16,128]{2,1,0:T(8,128)S(1)}, f32[1,16,128]{2,1,0:T(8,128)S(1)}, u32[]{:S(2)}, u32[]{:S(2)}) collective-permute-start(f32[1,16,128]{2,1,0:T(8,128)S(1)} %bitcast.675), channel_id=1, source_target_pairs={{0,1},{1,2},{2,3},{3,4},{4,5},{5,6},{6,7},{7,8},{8,9},{9,10},{10,1... | collective-permute-start | bytes 24584 | tf_op jit(solution)/shard_map/ppermute | solution.py:23
  254.8 4.5 collective-permute-start.19
  307.0 6.0 collective-permute-start.21
  310.9 9.8 %collective-permute-start.20 = (f32[1,16,128]{2,1,0:T(8,128)S(1)}, f32[1,16,128]{2,1,0:T(8,128)S(1)}, u32[]{:S(2)}, u32[]{:S(2)}) collective-permute-start(f32[1,16,128]{2,1,0:T(8,128)S(1)} %bitcast.668), channel_id=1, source_target_pairs={{0,1},{1,2},{2,3},{3,4},{4,5},{5,6},{6,7},{7,8},{8,9},{9,10},{10,1... | collective-permute-start | bytes 24584 | tf_op jit(solution)/shard_map/ppermute | solution.py:23
  330.8 4.4 collective-permute-start.23
  340.5 5.5 collective-permute-start.25
  346.1 9.8 %collective-permute-start.24 = (f32[1,16,128]{2,1,0:T(8,128)S(1)}, f32[1,16,128]{2,1,0:T(8,128)S(1)}, u32[]{:S(2)}, u32[]{:S(2)}) collective-permute-start(f32[1,16,128]{2,1,0:T(8,128)S(1)} %bitcast.676), channel_id=1, source_target_pairs={{0,1},{1,2},{2,3},{3,4},{4,5},{5,6},{6,7},{7,8},{8,9},{9,10},{10,1... | collective-permute-start | bytes 24584 | tf_op jit(solution)/shard_map/ppermute | solution.py:23
  364.4 5.0 collective-permute-start.26
  367.3 4.9 collective-permute-start.27
  421.0 6.1 collective-permute-start.29
  427.2 10.0 %collective-permute-start.28 = (f32[1,16,128]{2,1,0:T(8,128)S(1)}, f32[1,16,128]{2,1,0:T(8,128)S(1)}, u32[]{:S(2)}, u32[]{:S(2)}) collective-permute-start(f32[1,16,128]{2,1,0:T(8,128)S(1)} %bitcast.670), channel_id=1, source_target_pairs={{0,1},{1,2},{2,3},{3,4},{4,5},{5,6},{6,7},{7,8},{8,9},{9,10},{10,1... | collective-permute-start | bytes 24584 | tf_op jit(solution)/shard_map/ppermute | solution.py:23
  445.8 3.5 collective-permute-start.30
  447.1 4.4 collective-permute-start.31
  503.5 5.5 collective-permute-start.33
  509.1 9.8 %collective-permute-start.32 = (f32[1,16,128]{2,1,0:T(8,128)S(1)}, f32[1,16,128]{2,1,0:T(8,128)S(1)}, u32[]{:S(2)}, u32[]{:S(2)}) collective-permute-start(f32[1,16,128]{2,1,0:T(8,128)S(1)} %bitcast.669), channel_id=1, source_target_pairs={{0,1},{1,2},{2,3},{3,4},{4,5},{5,6},{6,7},{7,8},{8,9},{9,10},{10,1... | collective-permute-start | bytes 24584 | tf_op jit(solution)/shard_map/ppermute | solution.py:23
  528.7 4.4 collective-permute-start.35
  (178 other events, 2178.7 us)
where the time goes:
time: 631 us; the launch traced here: 619 us
  blocking collectives  285 us (45%)
  local copies, waits for them, and re-layouts  105 us (17%)
  starting transfers between devices  91.2 us (14%)
  waiting for transfers between devices  87.5 us (14%)
  between operations  24.2 us (4%)
  matrix products  13.4 us (2%)
  other arithmetic  12.3 us (2%)
    psum x35, blocking collectives, by_axis(): value = lax.psum(value, axis)  285 us
    ppermute x18, waiting for transfers between devices, with_halo(): lax.ppermute(lax.slice_in_dim(block, block.shape[dim] - width, None, axis...  53.2 us
    ppermute x18, starting transfers between devices, with_halo(): lax.ppermute(lax.slice_in_dim(block, 0, width, axis=dim), axis, backward)  47 us
    ppermute x18, starting transfers between devices, with_halo(): lax.ppermute(lax.slice_in_dim(block, block.shape[dim] - width, None, axis...  44.2 us
    unnamed x394, local copies, waits for them, and re-layouts  38.5 us
    slice x18, local copies, waits for them, and re-layouts, pair_sum(): lax.slice_in_dim(slot_first, 0, 1, axis=dim_index)  36.3 us
    ppermute x18, waiting for transfers between devices, with_halo(): lax.ppermute(lax.slice_in_dim(block, 0, width, axis=dim), axis, backward)  34.4 us
  transfers between devices with their start and end apart: 36, of which 22 were waited for; matrix products, arithmetic and copies ran while one was open for 3% of the time, Pallas kernels for 0%

commit v1 on v0

v1 whole, which is shorter than its diff:
```python
import functools

import jax
import jax.numpy as jnp
import numpy as np
from jax import lax
from jax.experimental import pallas as pl
from jax.experimental.pallas import tpu as pltpu
from jax.sharding import PartitionSpec as P

MESH = pl.DeviceIdType.MESH
HIGH = lax.Precision.HIGHEST
INV_STEP = 20.0
SHIFT = 0.75
FIELDS = (3, 1, 1, 1, 1)
STARTS = (0, 3, 4, 5, 6)
TOTAL = 7


def gll_tables():
    points = np.array(
        [
            -1.0,
            -0.8717401485096066,
            -0.5917001814331423,
            -0.2092992179024789,
            0.2092992179024789,
            0.5917001814331423,
            0.8717401485096066,
            1.0,
        ]
    )
    weights = np.array(
        [
            1.0 / 28.0,
            0.2107042271435061,
            0.3411226924835044,
            0.4124587946587038,
            0.4124587946587038,
            0.3411226924835044,
            0.2107042271435061,
            1.0 / 28.0,
        ]
    )
    product = np.array(
        [
            np.prod([points[column] - points[others] for others in range(8) if others != column])
            for column in range(8)
        ]
    )
    derivative = np.zeros((8, 8))
    for row_idx in range(8):
        for col_idx in range(8):
            if row_idx != col_idx:
                derivative[row_idx, col_idx] = product[row_idx] / (
                    product[col_idx] * (points[row_idx] - points[col_idx])
                )
        derivative[row_idx, row_idx] = -np.sum(derivative[row_idx])
    return derivative, weights


def tables():
    derivative, weights = gll_tables()
    stiff = derivative.T @ np.diag(weights) @ derivative
    scaled = stiff / weights[:, None]
    eye8, eye2, eye16 = np.eye(8), np.eye(2), np.eye(16)
    rows = np.kron(eye2, np.kron(scaled, eye8) + np.kron(eye8, scaled))
    lanes = np.kron(eye16, scaled.T)
    face = weights[:, None] * np.tile(weights, 16)[None, :]
    slope = np.diag(scaled)
    face_slope = slope[:, None] + np.tile(slope, 16)[None, :]
    const = np.concatenate([rows, lanes, face, face_slope]).astype(np.float32)
    return const, weights, slope


def kernel(
    shape,
    weights,
    slope,
    cot_ref,
    kap_ref,
    cap_ref,
    src_ref,
    const_ref,
    second_ref,
    first_ref,
    grad_ref,
    y_ref,
    face_ref,
    plane_in,
    height_in,
    work_ref,
    mat_ref,
    tile_a,
    tile_b,
    send_sem,
    recv_sem,
    send_red,
    recv_red,
):
    heights, planes = shape
    runs = 2
    per_run = planes // runs
    stack = heights * runs
    h = lax.axis_index("height")
    p = lax.axis_index("plane")
    run = p // per_run
    pos = lax.rem(p, per_run)
    level = h * runs + run
    h_lo, h_hi = lax.rem(h + heights - 1, heights), lax.rem(h + 1, heights)
    p_lo, p_hi = lax.rem(p + planes - 1, planes), lax.rem(p + 1, planes)

    def run_peer(step):
        return (h, run * per_run + lax.rem(pos + step, per_run))

    def stack_peer(step):
        other = lax.rem(level + step, stack)
        return (other // runs, lax.rem(other, runs) * per_run + pos)

    halo = (
        (h, p_lo),
        (h, p_hi),
        (h_lo, p),
        (h_hi, p),
        (h_lo, p_lo),
        (h_lo, p_hi),
        (h_hi, p_lo),
        (h_hi, p_hi),
    )
    barrier = pltpu.get_barrier_semaphore()
    for device in halo:
        pl.semaphore_signal(barrier, inc=1, device_id=device, device_id_type=MESH)

    def greet_run(step, carry):
        pl.semaphore_signal(barrier, inc=1, device_id=run_peer(step), device_id_type=MESH)
        return carry

    def greet_stack(step, carry):
        pl.semaphore_signal(barrier, inc=1, device_id=stack_peer(step), device_id_type=MESH)
        return carry

    lax.fori_loop(1, per_run, greet_run, 0)
    lax.fori_loop(1, stack, greet_stack, 0)

    has_p_lo = jnp.where(p > 0, 1.0, 0.0)
    has_p_hi = jnp.where(p < planes - 1, 1.0, 0.0)
    has_h_lo = jnp.where(h > 0, 1.0, 0.0)
    has_h_hi = jnp.where(h < heights - 1, 1.0, 0.0)

    lane = lax.broadcasted_iota(jnp.int32, (8, 128), 1)
    sub = lax.broadcasted_iota(jnp.int32, (8, 128), 0)
    lane_mod = lax.rem(lane, 8)
    opening = jnp.where((lane_mod == 0) & (lane > 0), 1.0, 0.0)
    ending = jnp.where((lane_mod == 7) & (lane < 127), 1.0, 0.0)
    row_first = jnp.where(sub == 0, 1.0, 0.0)
    row_last = jnp.where(sub == 7, 1.0, 0.0)

    spread = jnp.where(
        lax.broadcasted_iota(jnp.int32, (16, 128), 1) // 8
        == lax.broadcasted_iota(jnp.int32, (16, 128), 0),
        1.0,
        0.0,
    )
    elems = jnp.concatenate([kap_ref[0], kap_ref[1], cap_ref[0], cap_ref[1]] * 2, axis=0)
    wide = jnp.dot(elems, spread, precision=HIGH, preferred_element_type=jnp.float32)
    face_w = const_ref[256:264, :]
    face_slope = const_ref[264:272, :]
    stiff_w = [face_w * wide[e : e + 1, :] for e in range(2)]
    mass_w = [face_w * (INV_STEP * wide[2 + e : 3 + e, :]) for e in range(2)]

    def put(slot, values):
        y_ref[slot] = values
        flat = values.reshape(128, 128)
        work_ref[slot] = flat
        for side, row in ((0, 0), (1, 7)):
            face_ref[side, slot] = work_ref.at[slot][pl.ds(row, 16, stride=8), :]

    def copies(index):
        slots = pl.ds(STARTS[index], FIELDS[index])
        routes = (
            (face_ref.at[0, slots], plane_in.at[1, slots]),
            (face_ref.at[1, slots], plane_in.at[0, slots]),
            (y_ref.at[slots, 0], height_in.at[1, slots]),
            (y_ref.at[slots, 15], height_in.at[0, slots]),
            (y_ref.at[slots, 0], height_in.at[5, slots]),
            (y_ref.at[slots, 0], height_in.at[4, slots]),
            (y_ref.at[slots, 15], height_in.at[3, slots]),
            (y_ref.at[slots, 15], height_in.at[2, slots]),
        )
        return [
            pltpu.make_async_remote_copy(
                src_ref=source,
                dst_ref=target,
                send_sem=send_sem.at[index, way],
                recv_sem=recv_sem.at[index, way],
                device_id=halo[way],
                device_id_type=MESH,
            )
            for way, (source, target) in enumerate(routes)
        ]

    def gathered(slot):
        work = work_ref.at[slot]
        work[pl.ds(0, 16, stride=8), :] += has_p_lo * plane_in[0, slot]
        work[pl.ds(7, 16, stride=8), :] += has_p_hi * plane_in[1, slot]
        low = (
            height_in[0, slot]
            + (row_first * has_p_lo) * pltpu.roll(height_in[2, slot], 1, axis=0)
            + (row_last * has_p_hi) * pltpu.roll(height_in[3, slot], 7, axis=0)
        )
        high = (
            height_in[1, slot]
            + (row_first * has_p_lo) * pltpu.roll(height_in[4, slot], 1, axis=0)
            + (row_last * has_p_hi) * pltpu.roll(height_in[5, slot], 7, axis=0)
        )
        work[0:8, :] += has_h_lo * low
        work[120:128, :] += has_h_hi * high
        joined = work[56:64, :] + work[64:72, :]
        work[56:64, :] = joined
        work[64:72, :] = joined
        flat = work[...]
        after = pltpu.roll(flat, 127, axis=1).reshape(16, 8, 128)
        before = pltpu.roll(flat, 1, axis=1).reshape(16, 8, 128)
        return flat.reshape(16, 8, 128) + ending[None] * after + opening[None] * before

    def layered(parts):
        return jnp.stack([weights[a] * parts[e] for e in range(2) for a in range(8)])

    mass = layered(mass_w)
    conduct = layered(stiff_w)
    slopes = jnp.stack([face_slope + slope[a] for a in range(8)] * 2)

    def stiffness(values):
        flat = values.reshape(128, 128)
        inner = jnp.dot(
            const_ref[0:128, :], flat, precision=HIGH, preferred_element_type=jnp.float32
        ) + jnp.dot(flat, const_ref[128:256, :], precision=HIGH, preferred_element_type=jnp.float32)
        return mat_ref[0] * values + mat_ref[1] * inner.reshape(16, 8, 128)

    mat_ref[0] = mass
    mat_ref[1] = conduct
    put(0, mass * cot_ref[...])
    put(1, mass)
    put(2, mass + conduct * slopes)

    pl.semaphore_wait(barrier, 8 + per_run - 1 + stack - 1)

    started = []

    def send(index):
        batch = copies(index)
        for copy in batch:
            copy.start()
        started.append(batch)

    def arrive(index):
        for copy in started[index]:
            copy.wait_recv()

    send(0)

    local = lax.broadcasted_iota(jnp.int32, (128, 128), 0) // 8
    hits = []
    for step in range(2):
        wanted = src_ref[step : step + 1, :]
        hits.append(
            jnp.concatenate(
                [
                    jnp.where(wanted == ((h * 2 + e) * planes + p) * 16 + local, 1.0, 0.0)
                    for e in range(2)
                ],
                axis=0,
            )
        )

    def source_sums(fields, hit):
        rows = []
        for values in fields:
            weighed = mat_ref[0] * values
            rows.append(
                jnp.concatenate(
                    [
                        jnp.sum(weighed[8 * e : 8 * e + 8].reshape(64, 128), axis=0, keepdims=True)
                        for e in range(2)
                    ],
                    axis=1,
                )
            )
        rows = jnp.concatenate(rows + [jnp.zeros((5, 256), jnp.float32)], axis=0)
        return jnp.dot(rows, hit, precision=HIGH, preferred_element_type=jnp.float32)

    depth_copies = [jnp.ones((1, 1), jnp.float32)] * 16
    depth_copies[0] = jnp.full((1, 1), 1.0 / (1.0 + has_h_lo))
    depth_copies[7] = depth_copies[8] = jnp.full((1, 1), 0.5)
    depth_copies[15] = jnp.full((1, 1), 1.0 / (1.0 + has_h_hi))
    plane_copies = (
        1.0 / ((1.0 + row_first * has_p_lo + row_last * has_p_hi) * (1.0 + opening + ending))
    )

    arrive(0)
    diag = gathered(2)
    inv_diag = 1.0 / diag
    mat_ref[2] = inv_diag
    mat_ref[3] = jnp.stack([diag[i] * plane_copies * depth_copies[i] for i in range(16)])
    mat_ref[4] = gathered(1) * inv_diag

    def dot_rows(left, right):
        return jnp.sum((left * right).reshape(128, 128), axis=0, keepdims=True)

    def total(index, tile):
        for stage, (ref, spot, count, peer) in enumerate(
            ((tile_a, pos, per_run, run_peer), (tile_b, level, stack, stack_peer))
        ):
            own = ref.at[index, spot]
            own[...] = tile

            def push(step, carry):
                pltpu.make_async_remote_copy(
                    src_ref=own,
                    dst_ref=own,
                    send_sem=send_red.at[index, stage],
                    recv_sem=recv_red.at[index, stage],
                    device_id=peer(step),
                    device_id_type=MESH,
                ).start()
                return carry

            lax.fori_loop(1, count, push, 0)
            rest = ref.at[index, pl.ds(0, count - 1)]
            waiter = pltpu.make_async_remote_copy(
                src_ref=rest,
                dst_ref=rest,
                send_sem=send_red.at[index, stage],
                recv_sem=recv_red.at[index, stage],
                device_id=peer(1),
                device_id_type=MESH,
            )
            waiter.wait_send()
            waiter.wait_recv()
            tile = jnp.sum(ref[index], axis=0)
        return tile

    def solve(index, first, hit):
        base = 2 * index + 1
        applied = stiffness(first)
        put(STARTS[base], applied)
        send(base)
        weighted = mat_ref[3]
        arrive(base)
        second = gathered(STARTS[base]) * mat_ref[2] - SHIFT * first
        applied = stiffness(second)
        put(STARTS[base + 1], applied)
        send(base + 1)
        m = [dot_rows(weighted * first, first), dot_rows(weighted * first, second)]
        m.append(dot_rows(weighted * second, second))
        arrive(base + 1)
        third = gathered(STARTS[base + 1]) * mat_ref[2] - SHIFT * second
        m.append(dot_rows(weighted * second, third))
        m.append(dot_rows(weighted * third, third))
        m.append(dot_rows(third, stiffness(third)) - SHIFT * m[4])
        basis = (first, second, third)
        tile = jnp.concatenate(
            m + [jnp.zeros((2, 128), jnp.float32), source_sums(basis, hit)], axis=0
        )
        tile = total(index, tile)
        m = jnp.broadcast_to(jnp.sum(tile[0:8], axis=1, keepdims=True), (8, 128))
        m = [m[k : k + 1] for k in range(6)]
        a = [m[k + 1] + SHIFT * m[k] for k in range(5)]
        pivot0 = a[0]
        l1 = a[1] / pivot0
        l2 = a[2] / pivot0
        pivot1 = a[2] - l1 * a[1]
        cross = a[3] - l1 * a[2]
        inv1 = jnp.where(pivot1 > 1e-7 * a[2], 1.0 / pivot1, 0.0)
        l12 = cross * inv1
        pivot2 = a[4] - l2 * a[2] - l12 * cross
        inv2 = jnp.where(pivot2 > 1e-7 * a[4], 1.0 / pivot2, 0.0)
        g1 = m[1] - l1 * m[0]
        g2 = m[2] - l2 * m[0] - l12 * g1
        c2 = g2 * inv2
        c1 = g1 * inv1 - l12 * c2
        c0 = m[0] / pivot0 - l1 * c1 - l2 * c2
        answer = c0[None] * first + c1[None] * second + c2[None] * third
        grads = c0 * tile[8:9] + c1 * tile[9:10] + c2 * tile[10:11]
        return answer, grads * (1.0 / (8.0 * INV_STEP))

    later, later_grad = solve(0, gathered(0) * inv_diag, hits[1])
    second_ref[...] = later
    earlier, earlier_grad = solve(1, later * mat_ref[4], hits[0])
    first_ref[...] = earlier
    grad_ref[0:1, :] = earlier_grad
    grad_ref[1:2, :] = later_grad
    for batch in started:
        for copy in batch:
            copy.wait_send()


def solution(mesh):
    shape = (mesh.shape["height"], mesh.shape["plane"])
    const, weights, slope = tables()
    weights = [float(value) for value in weights]
    slope = [float(value) for value in slope]
    run, stack = shape[1] // 2, shape[0] * 2

    def per_device(cotangent, conductivity, capacity, sources):
        block = jax.ShapeDtypeStruct(cotangent.shape, jnp.float32)
        return pl.pallas_call(
            functools.partial(kernel, shape, weights, slope),
            out_shape=(block, block, jax.ShapeDtypeStruct(sources.shape, jnp.float32)),
            in_specs=[pl.BlockSpec(memory_space=pltpu.VMEM)] * 5,
            out_specs=(pl.BlockSpec(memory_space=pltpu.VMEM),) * 3,
            scratch_shapes=[
                pltpu.VMEM((TOTAL, 16, 8, 128), jnp.float32),
                pltpu.VMEM((2, TOTAL, 16, 128), jnp.float32),
                pltpu.VMEM((2, TOTAL, 16, 128), jnp.float32),
                pltpu.VMEM((6, TOTAL, 8, 128), jnp.float32),
                pltpu.VMEM((TOTAL, 128, 128), jnp.float32),
                pltpu.VMEM((5, 16, 8, 128), jnp.float32),
                pltpu.VMEM((2, run, 16, 128), jnp.float32),
                pltpu.VMEM((2, stack, 16, 128), jnp.float32),
                pltpu.SemaphoreType.DMA((5, 8)),
                pltpu.SemaphoreType.DMA((5, 8)),
                pltpu.SemaphoreType.DMA((2, 2)),
                pltpu.SemaphoreType.DMA((2, 2)),
            ],
            compiler_params=pltpu.CompilerParams(collective_id=0, has_side_effects=True),
        )(cotangent, conductivity, capacity, sources, jnp.asarray(const))

    split = P("height", "plane", None)
    return jax.shard_map(
        per_device,
        mesh=mesh,
        in_specs=(split, split, split, P(None, None)),
        out_specs=(split, split, P(None, None)),
        check_vma=False,
    )
```

time: 631 us -> 68.4 us (0.11)
  the two profiles are of different devices: /device:TPU:32 before, /device:TPU:1 now
where the time goes in v1:
time: 68.4 us; the launch traced here: 68.2 us
  Pallas kernels  64.8 us (95%)
  local copies, waits for them, and re-layouts  2.71 us (4%)
    pallas_call x1, Pallas kernels, per_device(): pl.pallas_call(functools.partial(kernel, shape, weights, slope), out_shap...  64.8 us
    unnamed x7, local copies, waits for them, and re-layouts  2.71 us

profile of v1, /device:TPU:1, one launch (start us, length us, event | category | flops | bytes accessed | tf_op | source)
XLA Modules:
  0.0 68.2 jit_solution(7444336879176795064)
XLA Ops:
  0.6 64.8 %shard_map.76 = (f32[16,8,128]{2,1,0:T(8,128)}, f32[16,8,128]{2,1,0:T(8,128)}, f32[2,128]{1,0:T(2,128)}) custom-call(f32[16,8,128]{2,1,0:T(8,128)} %cot_ref.1, f32[2,1,16]{2,1,0:T(1,128)} %kap_ref.1, f32[2,1,16]{2,1,0:T(1,128)} %cap_ref.1, s32[2,128]{1,0:T(2,128)} %src_ref.1, f32[272,128]{1,0:T(8,128)} %constant.2.clone.const_ref), custom_call_target="tpu_custom_call" | custom-call | tf_op jit(solution)/shard_map/pallas_call | solution.py:407
  65.5 0.0 copy-start
  65.5 1.5 %copy.11 = f32[16,8,128]{2,1,0:T(8,128)} copy(f32[16,8,128]{2,1,0:T(8,128)} %get-tuple-element.6) | data formatting | bytes 131072
  67.0 0.0 copy-done
  67.0 0.0 copy-start.1
  67.0 0.6 copy.12
  67.6 0.0 copy-done.1
  67.6 0.6 copy.13
Async XLA Ops:
  65.5 1.5 %copy-start = (f32[16,8,128]{2,1,0:T(8,128)S(1)}, f32[16,8,128]{2,1,0:T(8,128)}, u32[]{:S(2)}) copy-start(f32[16,8,128]{2,1,0:T(8,128)} %get-tuple-element.7) | copy-start | bytes 196612
  67.0 0.6 copy-start.1

commit v2 on v1

--- a/solution.py
+++ b/solution.py
@@ -85,6 +85,10 @@
     second_ref,
     first_ref,
     grad_ref,
+    home_ref,
+    moved_ref,
+    back_ref,
+    out_ref,
     y_ref,
     face_ref,
     plane_in,
@@ -97,35 +101,62 @@
     recv_sem,
     send_red,
     recv_red,
+    send_move,
+    recv_move,
 ):
-    heights, planes = shape
+    heights, planes = shape[:2]
     runs = 2
     per_run = planes // runs
     stack = heights * runs
-    h = lax.axis_index("height")
-    p = lax.axis_index("plane")
-    run = p // per_run
-    pos = lax.rem(p, per_run)
-    level = h * runs + run
+    high = lax.axis_index("height")
+    wide = lax.axis_index("plane")
+    run = wide // per_run
+    pos = lax.rem(wide, per_run)
+    level = high * runs + run
+    side = shape[2]
+    rows_per_run = per_run // side
+
+    def host(block_h, block_p):
+        half = block_p // per_run
+        row = lax.rem(block_p, per_run) // side
+        column = lax.rem(block_p, side)
+        column = column + lax.rem(row, 2) * (side - 1 - 2 * column)
+        row = row + half * (rows_per_run - 1 - 2 * row)
+        pair = block_h // 2
+        return (2 * pair + half, lax.rem(block_h, 2) * per_run + row * side + column)
+
+    half = lax.rem(high, 2)
+    row = pos // side
+    column = lax.rem(pos, side)
+    row = row + half * (rows_per_run - 1 - 2 * row)
+    column = column + lax.rem(row, 2) * (side - 1 - 2 * column)
+    h = 2 * (high // 2) + run
+    p = half * per_run + row * side + column
+    target = host(high, wide)
+    source = (h, p)
+    moves = jnp.logical_or(h != high, p != wide)
     h_lo, h_hi = lax.rem(h + heights - 1, heights), lax.rem(h + 1, heights)
     p_lo, p_hi = lax.rem(p + planes - 1, planes), lax.rem(p + 1, planes)
 
     def run_peer(step):
-        return (h, run * per_run + lax.rem(pos + step, per_run))
+        return (high, run * per_run + lax.rem(pos + step, per_run))
 
     def stack_peer(step):
         other = lax.rem(level + step, stack)
         return (other // runs, lax.rem(other, runs) * per_run + pos)
 
-    halo = (
-        (h, p_lo),
-        (h, p_hi),
-        (h_lo, p),
-        (h_hi, p),
-        (h_lo, p_lo),
-        (h_lo, p_hi),
-        (h_hi, p_lo),
-        (h_hi, p_hi),
+    halo = tuple(
+        host(*block)
+        for block in (
+            (h, p_lo),
+            (h, p_hi),
+            (h_lo, p),
+            (h_hi, p),
+            (h_lo, p_lo),
+            (h_lo, p_hi),
+            (h_hi, p_lo),
+            (h_hi, p_hi),
+        )
     )
     barrier = pltpu.get_barrier_semaphore()
     for device in halo:
@@ -138,6 +169,11 @@
     def greet_stack(step, carry):
         pl.semaphore_signal(barrier, inc=1, device_id=stack_peer(step), device_id_type=MESH)
         return carry
+
+    @pl.when(moves)
+    def _():
+        pl.semaphore_signal(barrier, inc=1, device_id=target, device_id_type=MESH)
+        pl.semaphore_signal(barrier, inc=1, device_id=source, device_id_type=MESH)
 
     lax.fori_loop(1, per_run, greet_run, 0)
     lax.fori_loop(1, stack, greet_stack, 0)
@@ -162,11 +198,31 @@
         0.0,
     )
     elems = jnp.concatenate([kap_ref[0], kap_ref[1], cap_ref[0], cap_ref[1]] * 2, axis=0)
-    wide = jnp.dot(elems, spread, precision=HIGH, preferred_element_type=jnp.float32)
-    face_w = const_ref[256:264, :]
-    face_slope = const_ref[264:272, :]
-    stiff_w = [face_w * wide[e : e + 1, :] for e in range(2)]
-    mass_w = [face_w * (INV_STEP * wide[2 + e : 3 + e, :]) for e in range(2)]
+    home_ref[0:16] = cot_ref[...]
+    home_ref[16] = jnp.dot(elems, spread, precision=HIGH, preferred_element_type=jnp.float32)
+    greetings = 8 + per_run - 1 + stack - 1
+
+    def move(index, source_ref, target_ref, device):
+        return pltpu.make_async_remote_copy(
+            src_ref=source_ref,
+            dst_ref=target_ref,
+            send_sem=send_move.at[index],
+            recv_sem=recv_move.at[index],
+            device_id=device,
+            device_id_type=MESH,
+        )
+
+    bring = move(0, home_ref, moved_ref, target)
+
+    @pl.when(moves)
+    def _():
+        pl.semaphore_wait(barrier, greetings + 2)
+        bring.start()
+
+    @pl.when(jnp.logical_not(moves))
+    def _():
+        pl.semaphore_wait(barrier, greetings)
+        moved_ref[...] = home_ref[...]
 
     def put(slot, values):
         y_ref[slot] = values
@@ -226,6 +282,15 @@
     def layered(parts):
         return jnp.stack([weights[a] * parts[e] for e in range(2) for a in range(8)])
 
+    @pl.when(moves)
+    def _():
+        bring.wait_recv()
+
+    elems = moved_ref[16]
+    face_w = const_ref[256:264, :]
+    face_slope = const_ref[264:272, :]
+    stiff_w = [face_w * elems[e : e + 1, :] for e in range(2)]
+    mass_w = [face_w * (INV_STEP * elems[2 + e : 3 + e, :]) for e in range(2)]
     mass = layered(mass_w)
     conduct = layered(stiff_w)
     slopes = jnp.stack([face_slope + slope[a] for a in range(8)] * 2)
@@ -239,11 +304,9 @@
 
     mat_ref[0] = mass
     mat_ref[1] = conduct
-    put(0, mass * cot_ref[...])
+    put(0, mass * moved_ref[0:16])
     put(1, mass)
     put(2, mass + conduct * slopes)
-
-    pl.semaphore_wait(barrier, 8 + per_run - 1 + stack - 1)
 
     started = []
 
@@ -307,7 +370,7 @@
     def dot_rows(left, right):
         return jnp.sum((left * right).reshape(128, 128), axis=0, keepdims=True)
 
-    def total(index, tile):
+    def total(index, tile, between):
         for stage, (ref, spot, count, peer) in enumerate(
             ((tile_a, pos, per_run, run_peer), (tile_b, level, stack, stack_peer))
         ):
@@ -326,6 +389,8 @@
                 return carry
 
             lax.fori_loop(1, count, push, 0)
+            if between and stage == 0:
+                between()
             rest = ref.at[index, pl.ds(0, count - 1)]
             waiter = pltpu.make_async_remote_copy(
                 src_ref=rest,
@@ -340,17 +405,21 @@
             tile = jnp.sum(ref[index], axis=0)
         return tile
 
-    def solve(index, first, hit):
+    def solve(index, first, hit, keep):
         base = 2 * index + 1
         applied = stiffness(first)
         put(STARTS[base], applied)
         send(base)
+        if keep:
+            keep(1, first)
         weighted = mat_ref[3]
         arrive(base)
         second = gathered(STARTS[base]) * mat_ref[2] - SHIFT * first
         applied = stiffness(second)
         put(STARTS[base + 1], applied)
         send(base + 1)
+        if keep:
+            keep(2, second)
         m = [dot_rows(weighted * first, first), dot_rows(weighted * first, second)]
         m.append(dot_rows(weighted * second, second))
         arrive(base + 1)
@@ -359,12 +428,17 @@
         m.append(dot_rows(weighted * third, third))
         m.append(dot_rows(third, stiffness(third)) - SHIFT * m[4])
         basis = (first, second, third)
-        tile = jnp.concatenate(
-            m + [jnp.zeros((2, 128), jnp.float32), source_sums(basis, hit)], axis=0
-        )
-        tile = total(index, tile)
-        m = jnp.broadcast_to(jnp.sum(tile[0:8], axis=1, keepdims=True), (8, 128))
-        m = [m[k : k + 1] for k in range(6)]
+        m = [part + pltpu.roll(part, 64, axis=1) for part in m]
+        m = [jnp.where(lane[0:1] < 64, m[2 * k], m[2 * k + 1]) for k in range(3)]
+        sums = source_sums(basis, hit)
+        tile = jnp.concatenate(m + [sums[0:3], jnp.zeros((2, 128), jnp.float32)], axis=0)
+        tile = total(index, tile, (lambda: keep(3, third)) if keep else None)
+        left = jnp.where(lane < 64, tile, 0.0)
+        left_sum = jnp.broadcast_to(jnp.sum(left, axis=1, keepdims=True), (8, 128))
+        right_sum = jnp.broadcast_to(jnp.sum(tile - left, axis=1, keepdims=True), (8, 128))
+        m = [
+            (right_sum if k % 2 else left_sum)[k // 2 : k // 2 + 1] for k in range(6)
+        ]
         a = [m[k + 1] + SHIFT * m[k] for k in range(5)]
         pivot0 = a[0]
         l1 = a[1] / pivot0
@@ -380,23 +454,55 @@
         c2 = g2 * inv2
         c1 = g1 * inv1 - l12 * c2
         c0 = m[0] / pivot0 - l1 * c1 - l2 * c2
-        answer = c0[None] * first + c1[None] * second + c2[None] * third
-        grads = c0 * tile[8:9] + c1 * tile[9:10] + c2 * tile[10:11]
-        return answer, grads * (1.0 / (8.0 * INV_STEP))
-
-    later, later_grad = solve(0, gathered(0) * inv_diag, hits[1])
-    second_ref[...] = later
-    earlier, earlier_grad = solve(1, later * mat_ref[4], hits[0])
-    first_ref[...] = earlier
+        grads = c0 * tile[3:4] + c1 * tile[4:5] + c2 * tile[5:6]
+        return (c0[None], c1[None], c2[None]), grads * (1.0 / (8.0 * INV_STEP)), basis
+
+    def give_back(index):
+        send_back = move(1 + index, out_ref.at[index], back_ref.at[index], source)
+
+        @pl.when(moves)
+        def _():
+            send_back.start()
+
+        @pl.when(jnp.logical_not(moves))
+        def _():
+            back_ref[index] = out_ref[index]
+
+        return send_back
+
+    returns = []
+
+    def keep(index, values):
+        out_ref[index] = values
+        returns.append(give_back(index))
+
+    coef, later_grad, basis = solve(0, gathered(0) * inv_diag, hits[1], None)
+    later = coef[0] * basis[0] + coef[1] * basis[1] + coef[2] * basis[2]
+    keep(0, later)
+    coef, earlier_grad, _ = solve(1, later * mat_ref[4], hits[0], keep)
+    for send_back in returns:
+
+        @pl.when(moves)
+        def _():
+            send_back.wait_recv()
+
+    second_ref[...] = back_ref[0]
+    first_ref[...] = coef[0] * back_ref[1] + coef[1] * back_ref[2] + coef[2] * back_ref[3]
     grad_ref[0:1, :] = earlier_grad
     grad_ref[1:2, :] = later_grad
     for batch in started:
         for copy in batch:
             copy.wait_send()
 
+    @pl.when(moves)
+    def _():
+        bring.wait_send()
+        for send_back in returns:
+            send_back.wait_send()
+
 
 def solution(mesh):
-    shape = (mesh.shape["height"], mesh.shape["plane"])
+    shape = (mesh.shape["height"], mesh.shape["plane"], 4)
     const, weights, slope = tables()
     weights = [float(value) for value in weights]
     slope = [float(value) for value in slope]
@@ -410,18 +516,24 @@
             in_specs=[pl.BlockSpec(memory_space=pltpu.VMEM)] * 5,
             out_specs=(pl.BlockSpec(memory_space=pltpu.VMEM),) * 3,
             scratch_shapes=[
+                pltpu.VMEM((17, 8, 128), jnp.float32),
+                pltpu.VMEM((17, 8, 128), jnp.float32),
+                pltpu.VMEM((4, 16, 8, 128), jnp.float32),
+                pltpu.VMEM((4, 16, 8, 128), jnp.float32),
                 pltpu.VMEM((TOTAL, 16, 8, 128), jnp.float32),
                 pltpu.VMEM((2, TOTAL, 16, 128), jnp.float32),
                 pltpu.VMEM((2, TOTAL, 16, 128), jnp.float32),
                 pltpu.VMEM((6, TOTAL, 8, 128), jnp.float32),
                 pltpu.VMEM((TOTAL, 128, 128), jnp.float32),
                 pltpu.VMEM((5, 16, 8, 128), jnp.float32),
-                pltpu.VMEM((2, run, 16, 128), jnp.float32),
-                pltpu.VMEM((2, stack, 16, 128), jnp.float32),
+                pltpu.VMEM((2, run, 8, 128), jnp.float32),
+                pltpu.VMEM((2, stack, 8, 128), jnp.float32),
                 pltpu.SemaphoreType.DMA((5, 8)),
                 pltpu.SemaphoreType.DMA((5, 8)),
                 pltpu.SemaphoreType.DMA((2, 2)),
                 pltpu.SemaphoreType.DMA((2, 2)),
+                pltpu.SemaphoreType.DMA((5,)),
+                pltpu.SemaphoreType.DMA((5,)),
             ],
             compiler_params=pltpu.CompilerParams(collective_id=0, has_side_effects=True),
         )(cotangent, conductivity, capacity, sources, jnp.asarray(const))

time: 68.4 us -> 62.5 us (0.914)
  Pallas kernels: 64.8 us -> 59 us
    pallas_call x1, Pallas kernels: 64.8 us -> 59 us  [per_device(): pl.pallas_call(functools.partial(kernel, shape, weights, slope), out_shap...]
where the time goes in v2:
time: 62.5 us; the launch traced here: 62.4 us
  Pallas kernels  59 us (94%)
  local copies, waits for them, and re-layouts  2.71 us (4%)
  between operations  0.65 us (1%)
    pallas_call x1, Pallas kernels, per_device(): pl.pallas_call(functools.partial(kernel, shape, weights, slope), out_shap...  59 us
    unnamed x7, local copies, waits for them, and re-layouts  2.71 us

profile of v2, /device:TPU:1, one launch (start us, length us, event | category | flops | bytes accessed | tf_op | source)
XLA Modules:
  0.0 62.4 jit_solution(16318171509281831935)
XLA Ops:
  0.6 59.0 %shard_map.76 = (f32[16,8,128]{2,1,0:T(8,128)}, f32[16,8,128]{2,1,0:T(8,128)}, f32[2,128]{1,0:T(2,128)}) custom-call(f32[16,8,128]{2,1,0:T(8,128)} %cot_ref.1, f32[2,1,16]{2,1,0:T(1,128)} %kap_ref.1, f32[2,1,16]{2,1,0:T(1,128)} %cap_ref.1, s32[2,128]{1,0:T(2,128)} %src_ref.1, f32[272,128]{1,0:T(8,128)} %constant.2.clone.const_ref), custom_call_target="tpu_custom_call" | custom-call | tf_op jit(solution)/shard_map/pallas_call | solution.py:513
  59.7 0.0 copy-start
  59.7 1.5 %copy.11 = f32[16,8,128]{2,1,0:T(8,128)} copy(f32[16,8,128]{2,1,0:T(8,128)} %get-tuple-element.6) | data formatting | bytes 131072
  61.2 0.0 copy-done
  61.2 0.0 copy-start.1
  61.2 0.6 %copy.12 = f32[16,8,128]{2,1,0:T(8,128)} copy(f32[16,8,128]{2,1,0:T(8,128)S(1)} %copy-done) | data formatting | bytes 131072
  61.8 0.0 copy-done.1
  61.8 0.6 copy.13
Async XLA Ops:
  59.7 1.5 %copy-start = (f32[16,8,128]{2,1,0:T(8,128)S(1)}, f32[16,8,128]{2,1,0:T(8,128)}, u32[]{:S(2)}) copy-start(f32[16,8,128]{2,1,0:T(8,128)} %get-tuple-element.7) | copy-start | bytes 196612
  61.2 0.6 %copy-start.1 = (f32[2,128]{1,0:T(2,128)S(1)}, f32[2,128]{1,0:T(2,128)}, u32[]{:S(2)}) copy-start(f32[2,128]{1,0:T(2,128)} %get-tuple-element.8) | copy-start | bytes 3076

commit v3 on v2

--- a/solution.py
+++ b/solution.py
@@ -12,9 +12,9 @@
 HIGH = lax.Precision.HIGHEST
 INV_STEP = 20.0
 SHIFT = 0.75
-FIELDS = (3, 1, 1, 1, 1)
-STARTS = (0, 3, 4, 5, 6)
-TOTAL = 7
+FIELDS = (3, 1, 1, 3, 3)
+STARTS = (0, 3, 4, 5, 8)
+TOTAL = 11
 
 
 def gll_tables():
@@ -104,17 +104,17 @@
     send_move,
     recv_move,
 ):
-    heights, planes = shape[:2]
-    runs = 2
-    per_run = planes // runs
-    stack = heights * runs
+    heights, planes, side = shape
+    per_run = planes // 2
+    depth = heights
+    rows_per_run = per_run // side
     high = lax.axis_index("height")
     wide = lax.axis_index("plane")
     run = wide // per_run
     pos = lax.rem(wide, per_run)
-    level = high * runs + run
-    side = shape[2]
-    rows_per_run = per_run // side
+    core = lax.rem(high, 2)
+    level = 2 * (high // 2) + run
+    spot = 2 * level + core
 
     def host(block_h, block_p):
         half = block_p // per_run
@@ -125,25 +125,35 @@
         pair = block_h // 2
         return (2 * pair + half, lax.rem(block_h, 2) * per_run + row * side + column)
 
-    half = lax.rem(high, 2)
-    row = pos // side
-    column = lax.rem(pos, side)
-    row = row + half * (rows_per_run - 1 - 2 * row)
-    column = column + lax.rem(row, 2) * (side - 1 - 2 * column)
+    row_here = pos // side
+    column_here = lax.rem(pos, side)
+    row = row_here + core * (rows_per_run - 1 - 2 * row_here)
+    column = column_here + lax.rem(row, 2) * (side - 1 - 2 * column_here)
     h = 2 * (high // 2) + run
-    p = half * per_run + row * side + column
+    p = core * per_run + row * side + column
     target = host(high, wide)
     source = (h, p)
     moves = jnp.logical_or(h != high, p != wide)
     h_lo, h_hi = lax.rem(h + heights - 1, heights), lax.rem(h + 1, heights)
     p_lo, p_hi = lax.rem(p + planes - 1, planes), lax.rem(p + 1, planes)
 
-    def run_peer(step):
-        return (high, run * per_run + lax.rem(pos + step, per_run))
-
-    def stack_peer(step):
-        other = lax.rem(level + step, stack)
-        return (other // runs, lax.rem(other, runs) * per_run + pos)
+    def layer_peer(step):
+        other_row = lax.rem(row_here + step // side, rows_per_run)
+        other_column = lax.rem(column_here + step % side, side)
+        return (high, run * per_run + other_row * side + other_column)
+
+    def column_peer(step):
+        other = lax.rem(level + step // 2, depth)
+        other_core = lax.rem(core + step % 2, 2)
+        return (2 * (other // 2) + other_core, lax.rem(other, 2) * per_run + pos)
+
+    def far(offset, size):
+        return min(offset, size - offset)
+
+    layer_steps = sorted(
+        range(1, per_run), key=lambda k: -far(k // side, rows_per_run) - far(k % side, side)
+    )
+    column_steps = sorted(range(1, 2 * depth), key=lambda k: -far(k // 2, depth) - 0.1 * (k % 2))
 
     halo = tuple(
         host(*block)
@@ -162,12 +172,12 @@
     for device in halo:
         pl.semaphore_signal(barrier, inc=1, device_id=device, device_id_type=MESH)
 
-    def greet_run(step, carry):
-        pl.semaphore_signal(barrier, inc=1, device_id=run_peer(step), device_id_type=MESH)
+    def greet_layer(step, carry):
+        pl.semaphore_signal(barrier, inc=1, device_id=layer_peer(step), device_id_type=MESH)
         return carry
 
-    def greet_stack(step, carry):
-        pl.semaphore_signal(barrier, inc=1, device_id=stack_peer(step), device_id_type=MESH)
+    def greet_column(step, carry):
+        pl.semaphore_signal(barrier, inc=1, device_id=column_peer(step), device_id_type=MESH)
         return carry
 
     @pl.when(moves)
@@ -175,8 +185,8 @@
         pl.semaphore_signal(barrier, inc=1, device_id=target, device_id_type=MESH)
         pl.semaphore_signal(barrier, inc=1, device_id=source, device_id_type=MESH)
 
-    lax.fori_loop(1, per_run, greet_run, 0)
-    lax.fori_loop(1, stack, greet_stack, 0)
+    lax.fori_loop(1, per_run, greet_layer, 0)
+    lax.fori_loop(1, 2 * depth, greet_column, 0)
 
     has_p_lo = jnp.where(p > 0, 1.0, 0.0)
     has_p_hi = jnp.where(p < planes - 1, 1.0, 0.0)
@@ -200,7 +210,7 @@
     elems = jnp.concatenate([kap_ref[0], kap_ref[1], cap_ref[0], cap_ref[1]] * 2, axis=0)
     home_ref[0:16] = cot_ref[...]
     home_ref[16] = jnp.dot(elems, spread, precision=HIGH, preferred_element_type=jnp.float32)
-    greetings = 8 + per_run - 1 + stack - 1
+    greetings = 8 + per_run - 1 + 2 * depth - 1
 
     def move(index, source_ref, target_ref, device):
         return pltpu.make_async_remote_copy(
@@ -224,26 +234,23 @@
         pl.semaphore_wait(barrier, greetings)
         moved_ref[...] = home_ref[...]
 
-    def put(slot, values):
-        y_ref[slot] = values
-        flat = values.reshape(128, 128)
-        work_ref[slot] = flat
-        for side, row in ((0, 0), (1, 7)):
-            face_ref[side, slot] = work_ref.at[slot][pl.ds(row, 16, stride=8), :]
-
-    def copies(index):
+    started = []
+
+    def publish(index, fields):
         slots = pl.ds(STARTS[index], FIELDS[index])
+        first_rows = y_ref.at[slots, pl.ds(0, 8)]
+        last_rows = y_ref.at[slots, pl.ds(120, 8)]
         routes = (
             (face_ref.at[0, slots], plane_in.at[1, slots]),
             (face_ref.at[1, slots], plane_in.at[0, slots]),
-            (y_ref.at[slots, 0], height_in.at[1, slots]),
-            (y_ref.at[slots, 15], height_in.at[0, slots]),
-            (y_ref.at[slots, 0], height_in.at[5, slots]),
-            (y_ref.at[slots, 0], height_in.at[4, slots]),
-            (y_ref.at[slots, 15], height_in.at[3, slots]),
-            (y_ref.at[slots, 15], height_in.at[2, slots]),
-        )
-        return [
+            (first_rows, height_in.at[1, slots]),
+            (last_rows, height_in.at[0, slots]),
+            (first_rows, height_in.at[5, slots]),
+            (first_rows, height_in.at[4, slots]),
+            (last_rows, height_in.at[3, slots]),
+            (last_rows, height_in.at[2, slots]),
+        )
+        batch = [
             pltpu.make_async_remote_copy(
                 src_ref=source,
                 dst_ref=target,
@@ -254,6 +261,23 @@
             )
             for way, (source, target) in enumerate(routes)
         ]
+        started.append(batch)
+        for offset, values in enumerate(fields):
+            y_ref[STARTS[index] + offset] = values.reshape(128, 128)
+        for way in (4, 5, 6, 7, 2, 3):
+            batch[way].start()
+        for offset in range(FIELDS[index]):
+            slot = STARTS[index] + offset
+            for edge, row in ((0, 0), (1, 7)):
+                face_ref[edge, slot] = y_ref.at[slot][pl.ds(row, 16, stride=8), :]
+        for way in (0, 1):
+            batch[way].start()
+        for offset, values in enumerate(fields):
+            work_ref[STARTS[index] + offset] = values.reshape(128, 128)
+
+    def arrive(index):
+        for copy in started[index]:
+            copy.wait_recv()
 
     def gathered(slot):
         work = work_ref.at[slot]
@@ -295,32 +319,32 @@
     conduct = layered(stiff_w)
     slopes = jnp.stack([face_slope + slope[a] for a in range(8)] * 2)
 
-    def stiffness(values):
-        flat = values.reshape(128, 128)
-        inner = jnp.dot(
-            const_ref[0:128, :], flat, precision=HIGH, preferred_element_type=jnp.float32
-        ) + jnp.dot(flat, const_ref[128:256, :], precision=HIGH, preferred_element_type=jnp.float32)
-        return mat_ref[0] * values + mat_ref[1] * inner.reshape(16, 8, 128)
+    def stiffness(*fields):
+        flats = [values.reshape(128, 128) for values in fields]
+        across = jnp.dot(
+            const_ref[0:128, :],
+            jnp.concatenate(flats, axis=1),
+            precision=HIGH,
+            preferred_element_type=jnp.float32,
+        )
+        along = jnp.dot(
+            jnp.concatenate(flats, axis=0),
+            const_ref[128:256, :],
+            precision=HIGH,
+            preferred_element_type=jnp.float32,
+        )
+        return [
+            mat_ref[0] * values
+            + mat_ref[1]
+            * (
+                across[:, 128 * k : 128 * k + 128] + along[128 * k : 128 * k + 128]
+            ).reshape(16, 8, 128)
+            for k, values in enumerate(fields)
+        ]
 
     mat_ref[0] = mass
     mat_ref[1] = conduct
-    put(0, mass * moved_ref[0:16])
-    put(1, mass)
-    put(2, mass + conduct * slopes)
-
-    started = []
-
-    def send(index):
-        batch = copies(index)
-        for copy in batch:
-            copy.start()
-        started.append(batch)
-
-    def arrive(index):
-        for copy in started[index]:
-            copy.wait_recv()
-
-    send(0)
+    publish(0, (mass * moved_ref[0:16], mass, mass + conduct * slopes))
 
     local = lax.broadcasted_iota(jnp.int32, (128, 128), 0) // 8
     hits = []
@@ -370,75 +394,57 @@
     def dot_rows(left, right):
         return jnp.sum((left * right).reshape(128, 128), axis=0, keepdims=True)
 
-    def total(index, tile, between):
-        for stage, (ref, spot, count, peer) in enumerate(
-            ((tile_a, pos, per_run, run_peer), (tile_b, level, stack, stack_peer))
-        ):
-            own = ref.at[index, spot]
-            own[...] = tile
-
-            def push(step, carry):
-                pltpu.make_async_remote_copy(
-                    src_ref=own,
-                    dst_ref=own,
-                    send_sem=send_red.at[index, stage],
-                    recv_sem=recv_red.at[index, stage],
-                    device_id=peer(step),
-                    device_id_type=MESH,
-                ).start()
-                return carry
-
-            lax.fori_loop(1, count, push, 0)
-            if between and stage == 0:
-                between()
-            rest = ref.at[index, pl.ds(0, count - 1)]
-            waiter = pltpu.make_async_remote_copy(
-                src_ref=rest,
-                dst_ref=rest,
+    stages = (
+        (tile_a, pos, per_run, layer_peer, layer_steps),
+        (tile_b, spot, 2 * depth, column_peer, column_steps),
+    )
+
+    def push(index, stage, tile):
+        ref, slot, _, peer, steps = stages[stage]
+        own = ref.at[index, slot]
+        own[...] = tile
+        for step in steps:
+            pltpu.make_async_remote_copy(
+                src_ref=own,
+                dst_ref=own,
                 send_sem=send_red.at[index, stage],
                 recv_sem=recv_red.at[index, stage],
-                device_id=peer(1),
+                device_id=peer(step),
                 device_id_type=MESH,
-            )
-            waiter.wait_send()
-            waiter.wait_recv()
-            tile = jnp.sum(ref[index], axis=0)
-        return tile
-
-    def solve(index, first, hit, keep):
-        base = 2 * index + 1
-        applied = stiffness(first)
-        put(STARTS[base], applied)
-        send(base)
-        if keep:
-            keep(1, first)
-        weighted = mat_ref[3]
-        arrive(base)
-        second = gathered(STARTS[base]) * mat_ref[2] - SHIFT * first
-        applied = stiffness(second)
-        put(STARTS[base + 1], applied)
-        send(base + 1)
-        if keep:
-            keep(2, second)
+            ).start()
+
+    def rest(index, stage):
+        ref, _, count, peer, _ = stages[stage]
+        others = ref.at[index, pl.ds(0, count - 1)]
+        return pltpu.make_async_remote_copy(
+            src_ref=others,
+            dst_ref=others,
+            send_sem=send_red.at[index, stage],
+            recv_sem=recv_red.at[index, stage],
+            device_id=peer(1),
+            device_id_type=MESH,
+        )
+
+    def pull(index, stage):
+        rest(index, stage).wait_recv()
+        return jnp.sum(stages[stage][0][index], axis=0)
+
+    weighted = mat_ref[3]
+
+    def moments(first, second, third, applied):
         m = [dot_rows(weighted * first, first), dot_rows(weighted * first, second)]
         m.append(dot_rows(weighted * second, second))
-        arrive(base + 1)
-        third = gathered(STARTS[base + 1]) * mat_ref[2] - SHIFT * second
         m.append(dot_rows(weighted * second, third))
         m.append(dot_rows(weighted * third, third))
-        m.append(dot_rows(third, stiffness(third)) - SHIFT * m[4])
-        basis = (first, second, third)
+        m.append(dot_rows(third, applied) - SHIFT * m[4])
         m = [part + pltpu.roll(part, 64, axis=1) for part in m]
-        m = [jnp.where(lane[0:1] < 64, m[2 * k], m[2 * k + 1]) for k in range(3)]
-        sums = source_sums(basis, hit)
-        tile = jnp.concatenate(m + [sums[0:3], jnp.zeros((2, 128), jnp.float32)], axis=0)
-        tile = total(index, tile, (lambda: keep(3, third)) if keep else None)
+        return [jnp.where(lane[0:1] < 64, m[2 * k], m[2 * k + 1]) for k in range(3)]
+
+    def coefficients(tile):
         left = jnp.where(lane < 64, tile, 0.0)
         left_sum = jnp.broadcast_to(jnp.sum(left, axis=1, keepdims=True), (8, 128))
         right_sum = jnp.broadcast_to(jnp.sum(tile - left, axis=1, keepdims=True), (8, 128))
-        m = [
-            (right_sum if k % 2 else left_sum)[k // 2 : k // 2 + 1] for k in range(6)
-        ]
+        m = [(right_sum if k % 2 else left_sum)[k // 2 : k // 2 + 1] for k in range(6)]
         a = [m[k + 1] + SHIFT * m[k] for k in range(5)]
         pivot0 = a[0]
         l1 = a[1] / pivot0
@@ -454,10 +460,15 @@
         c2 = g2 * inv2
         c1 = g1 * inv1 - l12 * c2
         c0 = m[0] / pivot0 - l1 * c1 - l2 * c2
-        grads = c0 * tile[3:4] + c1 * tile[4:5] + c2 * tile[5:6]
-        return (c0[None], c1[None], c2[None]), grads * (1.0 / (8.0 * INV_STEP)), basis
-
-    def give_back(index):
+        return c0, c1, c2
+
+    def blend(coef, basis):
+        return coef[0] * basis[0] + coef[1] * basis[1] + coef[2] * basis[2]
+
+    returns = []
+
+    def keep(index, values):
+        out_ref[index] = values
         send_back = move(1 + index, out_ref.at[index], back_ref.at[index], source)
 
         @pl.when(moves)
@@ -468,28 +479,71 @@
         def _():
             back_ref[index] = out_ref[index]
 
-        return send_back
-
-    returns = []
-
-    def keep(index, values):
-        out_ref[index] = values
-        returns.append(give_back(index))
-
-    coef, later_grad, basis = solve(0, gathered(0) * inv_diag, hits[1], None)
-    later = coef[0] * basis[0] + coef[1] * basis[1] + coef[2] * basis[2]
+        returns.append(send_back)
+
+    def advance(index, previous):
+        arrive(index)
+        return [
+            gathered(STARTS[index] + k) * mat_ref[2] - SHIFT * values
+            for k, values in enumerate(previous)
+        ]
+
+    zeros = jnp.zeros((1, 128), jnp.float32)
+    v0 = gathered(0) * inv_diag
+    publish(1, stiffness(v0))
+    (v1,) = advance(1, (v0,))
+    publish(2, stiffness(v1))
+    (v2,) = advance(2, (v1,))
+    basis = (v0, v1, v2)
+    w0 = [values * mat_ref[4] for values in basis]
+    publish(3, stiffness(*w0))
+    sums = source_sums(basis, hits[1])
+    push(
+        0,
+        0,
+        jnp.concatenate(
+            moments(v0, v1, v2, stiffness(v2)[0]) + [sums[0:3], zeros, zeros], axis=0
+        ),
+    )
+    w1 = advance(3, w0)
+    publish(4, stiffness(*w1))
+    push(0, 1, pull(0, 0))
+    w2 = advance(4, w1)
+    tile = pull(0, 1)
+    coef = coefficients(tile)
+    later_grad = blend(coef, [tile[3 + k : 4 + k] for k in range(3)])
+    wide_coef = [c[None] for c in coef]
+    later = blend(wide_coef, basis)
+    basis = [blend(wide_coef, fields) for fields in (w0, w1, w2)]
+    sums = source_sums(basis, hits[0])
+    push(
+        1,
+        0,
+        jnp.concatenate(
+            moments(*basis, stiffness(basis[2])[0]) + [sums[0:3], zeros, zeros], axis=0
+        ),
+    )
     keep(0, later)
-    coef, earlier_grad, _ = solve(1, later * mat_ref[4], hits[0], keep)
-    for send_back in returns:
-
-        @pl.when(moves)
-        def _():
+    for k in range(3):
+        keep(1 + k, basis[k])
+    push(1, 1, pull(1, 0))
+    tile = pull(1, 1)
+    coef = coefficients(tile)
+    earlier_grad = blend(coef, [tile[3 + k : 4 + k] for k in range(3)])
+
+    @pl.when(moves)
+    def _():
+        for send_back in returns:
             send_back.wait_recv()
 
     second_ref[...] = back_ref[0]
-    first_ref[...] = coef[0] * back_ref[1] + coef[1] * back_ref[2] + coef[2] * back_ref[3]
-    grad_ref[0:1, :] = earlier_grad
-    grad_ref[1:2, :] = later_grad
+    first_ref[...] = blend([c[None] for c in coef], [back_ref[1 + k] for k in range(3)])
+    scale = 1.0 / (8.0 * INV_STEP)
+    grad_ref[0:1, :] = earlier_grad * scale
+    grad_ref[1:2, :] = later_grad * scale
+    for index in range(2):
+        for stage in range(2):
+            rest(index, stage).wait_send()
     for batch in started:
         for copy in batch:
             copy.wait_send()
@@ -520,7 +574,7 @@
                 pltpu.VMEM((17, 8, 128), jnp.float32),
                 pltpu.VMEM((4, 16, 8, 128), jnp.float32),
                 pltpu.VMEM((4, 16, 8, 128), jnp.float32),
-                pltpu.VMEM((TOTAL, 16, 8, 128), jnp.float32),
+                pltpu.VMEM((TOTAL, 128, 128), jnp.float32),
                 pltpu.VMEM((2, TOTAL, 16, 128), jnp.float32),
                 pltpu.VMEM((2, TOTAL, 16, 128), jnp.float32),
                 pltpu.VMEM((6, TOTAL, 8, 128), jnp.float32),

time: 62.5 us -> 56.4 us (0.902)
  Pallas kernels: 59 us -> 52.9 us
    pallas_call x1, Pallas kernels: 59 us -> 52.9 us  [per_device(): pl.pallas_call(functools.partial(kernel, shape, weights, slope), out_shap...]
where the time goes in v3:
time: 56.4 us; the launch traced here: 56.2 us
  Pallas kernels  52.9 us (94%)
  local copies, waits for them, and re-layouts  2.71 us (5%)
  between operations  0.65 us (1%)
    pallas_call x1, Pallas kernels, per_device(): pl.pallas_call(functools.partial(kernel, shape, weights, slope), out_shap...  52.9 us
    unnamed x7, local copies, waits for them, and re-layouts  2.71 us

profile of v3, /device:TPU:1, one launch (start us, length us, event | category | flops | bytes accessed | tf_op | source)
XLA Modules:
  0.0 56.2 jit_solution(6502392134670077700)
XLA Ops:
  0.6 52.9 %shard_map.76 = (f32[16,8,128]{2,1,0:T(8,128)}, f32[16,8,128]{2,1,0:T(8,128)}, f32[2,128]{1,0:T(2,128)}) custom-call(f32[16,8,128]{2,1,0:T(8,128)} %cot_ref.1, f32[2,1,16]{2,1,0:T(1,128)} %kap_ref.1, f32[2,1,16]{2,1,0:T(1,128)} %cap_ref.1, s32[2,128]{1,0:T(2,128)} %src_ref.1, f32[272,128]{1,0:T(8,128)} %constant.2.clone.const_ref), custom_call_target="tpu_custom_call" | custom-call | tf_op jit(solution)/shard_map/pallas_call | solution.py:567
  53.5 0.0 copy-start
  53.5 1.5 %copy.11 = f32[16,8,128]{2,1,0:T(8,128)} copy(f32[16,8,128]{2,1,0:T(8,128)} %get-tuple-element.6) | data formatting | bytes 131072
  55.0 0.0 copy-done
  55.0 0.0 copy-start.1
  55.0 0.6 %copy.12 = f32[16,8,128]{2,1,0:T(8,128)} copy(f32[16,8,128]{2,1,0:T(8,128)S(1)} %copy-done) | data formatting | bytes 131072
  55.7 0.0 copy-done.1
  55.7 0.6 copy.13
Async XLA Ops:
  53.5 1.5 %copy-start = (f32[16,8,128]{2,1,0:T(8,128)S(1)}, f32[16,8,128]{2,1,0:T(8,128)}, u32[]{:S(2)}) copy-start(f32[16,8,128]{2,1,0:T(8,128)} %get-tuple-element.7) | copy-start | bytes 196612
  55.0 0.6 %copy-start.1 = (f32[2,128]{1,0:T(2,128)S(1)}, f32[2,128]{1,0:T(2,128)}, u32[]{:S(2)}) copy-start(f32[2,128]{1,0:T(2,128)} %get-tuple-element.8) | copy-start | bytes 3076

commit v4 on v3

--- a/solution.py
+++ b/solution.py
@@ -77,14 +77,18 @@
     shape,
     weights,
     slope,
-    cot_ref,
+    cot_hbm,
+    kap_hbm,
+    cap_hbm,
+    src_hbm,
+    const_hbm,
+    second_ref,
+    first_ref,
+    grad_ref,
     kap_ref,
     cap_ref,
     src_ref,
     const_ref,
-    second_ref,
-    first_ref,
-    grad_ref,
     home_ref,
     moved_ref,
     back_ref,
@@ -103,7 +107,22 @@
     recv_red,
     send_move,
     recv_move,
+    load_sem,
 ):
+    loads = [
+        pltpu.make_async_copy(operand, place, load_sem.at[index])
+        for index, (operand, place) in enumerate(
+            (
+                (kap_hbm, kap_ref),
+                (cap_hbm, cap_ref),
+                (cot_hbm, home_ref.at[pl.ds(0, 16)]),
+                (const_hbm, const_ref),
+                (src_hbm, src_ref),
+            )
+        )
+    ]
+    for load in loads:
+        load.start()
     heights, planes, side = shape
     per_run = planes // 2
     depth = heights
@@ -207,9 +226,12 @@
         1.0,
         0.0,
     )
+    for load in loads[:2]:
+        load.wait()
     elems = jnp.concatenate([kap_ref[0], kap_ref[1], cap_ref[0], cap_ref[1]] * 2, axis=0)
-    home_ref[0:16] = cot_ref[...]
     home_ref[16] = jnp.dot(elems, spread, precision=HIGH, preferred_element_type=jnp.float32)
+    for load in loads[2:]:
+        load.wait()
     greetings = 8 + per_run - 1 + 2 * depth - 1
 
     def move(index, source_ref, target_ref, device):
@@ -555,6 +577,18 @@
             send_back.wait_send()
 
 
+def write_out(*refs):
+    sources, targets, sems = refs[:3], refs[3:6], refs[6]
+    stores = [
+        pltpu.make_async_copy(source, target, sems.at[index])
+        for index, (source, target) in enumerate(zip(sources, targets))
+    ]
+    for store in stores:
+        store.start()
+    for store in stores:
+        store.wait()
+
+
 def solution(mesh):
     shape = (mesh.shape["height"], mesh.shape["plane"], 4)
     const, weights, slope = tables()
@@ -564,12 +598,17 @@
 
     def per_device(cotangent, conductivity, capacity, sources):
         block = jax.ShapeDtypeStruct(cotangent.shape, jnp.float32)
-        return pl.pallas_call(
+        outs = (block, block, jax.ShapeDtypeStruct(sources.shape, jnp.float32))
+        results = pl.pallas_call(
             functools.partial(kernel, shape, weights, slope),
-            out_shape=(block, block, jax.ShapeDtypeStruct(sources.shape, jnp.float32)),
-            in_specs=[pl.BlockSpec(memory_space=pltpu.VMEM)] * 5,
+            out_shape=tuple(pltpu.VMEM(item.shape, item.dtype) for item in outs),
+            in_specs=[pl.BlockSpec(memory_space=pl.ANY)] * 5,
             out_specs=(pl.BlockSpec(memory_space=pltpu.VMEM),) * 3,
             scratch_shapes=[
+                pltpu.VMEM(conductivity.shape, jnp.float32),
+                pltpu.VMEM(capacity.shape, jnp.float32),
+                pltpu.VMEM(sources.shape, jnp.int32),
+                pltpu.VMEM(const.shape, jnp.float32),
                 pltpu.VMEM((17, 8, 128), jnp.float32),
                 pltpu.VMEM((17, 8, 128), jnp.float32),
                 pltpu.VMEM((4, 16, 8, 128), jnp.float32),
@@ -588,9 +627,17 @@
                 pltpu.SemaphoreType.DMA((2, 2)),
                 pltpu.SemaphoreType.DMA((5,)),
                 pltpu.SemaphoreType.DMA((5,)),
+                pltpu.SemaphoreType.DMA((5,)),
             ],
             compiler_params=pltpu.CompilerParams(collective_id=0, has_side_effects=True),
         )(cotangent, conductivity, capacity, sources, jnp.asarray(const))
+        return pl.pallas_call(
+            write_out,
+            out_shape=outs,
+            in_specs=[pl.BlockSpec(memory_space=pltpu.VMEM)] * 3,
+            out_specs=(pl.BlockSpec(memory_space=pl.ANY),) * 3,
+            scratch_shapes=[pltpu.SemaphoreType.DMA((3,))],
+        )(*[pltpu.with_memory_space_constraint(item, pltpu.VMEM) for item in results])
 
     split = P("height", "plane", None)
     return jax.shard_map(

time: 56.4 us -> 53.1 us (0.941)
  local copies, waits for them, and re-layouts: 2.71 us -> 0 us
  Pallas kernels: 52.9 us -> 52.3 us
    unnamed x7 -> x0, local copies, waits for them, and re-layouts: 2.71 us -> none
    pallas_call x1, Pallas kernels: 52.9 us -> 51.7 us  [per_device(): pl.pallas_call(functools.partial(kernel, shape, weights, slope), out_shap...]
    pallas_call x0 -> x1, Pallas kernels: none -> 0.68 us  [per_device(): pl.pallas_call(write_out, out_shape=outs, in_specs=[pl.BlockSpec(memory_s...]
where the time goes in v4:
time: 53.1 us; the launch traced here: 53 us
  Pallas kernels  52.3 us (98%)
  between operations  0.64 us (1%)
    pallas_call x1, Pallas kernels, per_device(): pl.pallas_call(functools.partial(kernel, shape, weights, slope), out_shap...  51.7 us

profile of v4, /device:TPU:1, one launch (start us, length us, event | category | flops | bytes accessed | tf_op | source)
XLA Modules:
  0.0 53.0 jit_solution(13103244960445122361)
XLA Ops:
  0.6 51.7 %shard_map.76 = (f32[16,8,128]{2,1,0:T(8,128)S(1)}, f32[16,8,128]{2,1,0:T(8,128)S(1)}, f32[2,128]{1,0:T(2,128)S(1)}) custom-call(f32[16,8,128]{2,1,0:T(8,128)} %cot_hbm.1, f32[2,1,16]{2,1,0:T(1,128)} %kap_hbm.1, f32[2,1,16]{2,1,0:T(1,128)} %cap_hbm.1, s32[2,128]{1,0:T(2,128)} %src_hbm.1, f32[272,128]{1,0:T(8,128)} %constant.2.clone.const_hbm), custom_call_target="tpu_custom_call" | custom-call | tf_op jit(solution)/shard_map/pallas_call | solution.py:602
  52.3 0.7 %shard_map.77 = (f32[16,8,128]{2,1,0:T(8,128)}, f32[16,8,128]{2,1,0:T(8,128)}, f32[2,128]{1,0:T(2,128)}) custom-call(f32[16,8,128]{2,1,0:T(8,128)S(1)} %get-tuple-element.6.refs_0_, f32[16,8,128]{2,1,0:T(8,128)S(1)} %get-tuple-element.7.refs_1_, f32[2,128]{1,0:T(2,128)S(1)} %get-tuple-element.8.refs_2_), custom_call_target="tpu_custom_call" | custom-call | tf_op jit(solution)/shard_map/pallas_call | solution.py:634

commit v5 on v4

--- a/solution.py
+++ b/solution.py
@@ -99,6 +99,8 @@
     height_in,
     work_ref,
     mat_ref,
+    row_a,
+    row_b,
     tile_a,
     tile_b,
     send_sem,
@@ -153,8 +155,6 @@
     target = host(high, wide)
     source = (h, p)
     moves = jnp.logical_or(h != high, p != wide)
-    h_lo, h_hi = lax.rem(h + heights - 1, heights), lax.rem(h + 1, heights)
-    p_lo, p_hi = lax.rem(p + planes - 1, planes), lax.rem(p + 1, planes)
 
     def layer_peer(step):
         other_row = lax.rem(row_here + step // side, rows_per_run)
@@ -174,21 +174,27 @@
     )
     column_steps = sorted(range(1, 2 * depth), key=lambda k: -far(k // 2, depth) - 0.1 * (k % 2))
 
-    halo = tuple(
-        host(*block)
-        for block in (
-            (h, p_lo),
-            (h, p_hi),
-            (h_lo, p),
-            (h_hi, p),
-            (h_lo, p_lo),
-            (h_lo, p_hi),
-            (h_hi, p_lo),
-            (h_hi, p_hi),
-        )
-    )
+    def around(block_h, block_p):
+        low_h = lax.rem(block_h + heights - 1, heights)
+        high_h = lax.rem(block_h + 1, heights)
+        low_p = lax.rem(block_p + planes - 1, planes)
+        high_p = lax.rem(block_p + 1, planes)
+        return (
+            (block_h, low_p),
+            (block_h, high_p),
+            (low_h, block_p),
+            (high_h, block_p),
+            (low_h, low_p),
+            (low_h, high_p),
+            (high_h, low_p),
+            (high_h, high_p),
+        )
+
+    halo = tuple(host(*block) for block in around(h, p))
+    entry_halo = tuple(host(*block) for block in around(high, wide))
+    remote = [jnp.logical_or(a != high, b != wide) for a, b in entry_halo]
     barrier = pltpu.get_barrier_semaphore()
-    for device in halo:
+    for device in halo + around(h, p) + (source,):
         pl.semaphore_signal(barrier, inc=1, device_id=device, device_id_type=MESH)
 
     def greet_layer(step, carry):
@@ -198,11 +204,6 @@
     def greet_column(step, carry):
         pl.semaphore_signal(barrier, inc=1, device_id=column_peer(step), device_id_type=MESH)
         return carry
-
-    @pl.when(moves)
-    def _():
-        pl.semaphore_signal(barrier, inc=1, device_id=target, device_id_type=MESH)
-        pl.semaphore_signal(barrier, inc=1, device_id=source, device_id_type=MESH)
 
     lax.fori_loop(1, per_run, greet_layer, 0)
     lax.fori_loop(1, 2 * depth, greet_column, 0)
@@ -232,7 +233,6 @@
     home_ref[16] = jnp.dot(elems, spread, precision=HIGH, preferred_element_type=jnp.float32)
     for load in loads[2:]:
         load.wait()
-    greetings = 8 + per_run - 1 + 2 * depth - 1
 
     def move(index, source_ref, target_ref, device):
         return pltpu.make_async_remote_copy(
@@ -246,19 +246,9 @@
 
     bring = move(0, home_ref, moved_ref, target)
 
-    @pl.when(moves)
-    def _():
-        pl.semaphore_wait(barrier, greetings + 2)
-        bring.start()
-
-    @pl.when(jnp.logical_not(moves))
-    def _():
-        pl.semaphore_wait(barrier, greetings)
-        moved_ref[...] = home_ref[...]
-
     started = []
 
-    def publish(index, fields):
+    def prepare(index, devices):
         slots = pl.ds(STARTS[index], FIELDS[index])
         first_rows = y_ref.at[slots, pl.ds(0, 8)]
         last_rows = y_ref.at[slots, pl.ds(120, 8)]
@@ -278,12 +268,16 @@
                 dst_ref=target,
                 send_sem=send_sem.at[index, way],
                 recv_sem=recv_sem.at[index, way],
-                device_id=halo[way],
+                device_id=devices[way],
                 device_id_type=MESH,
             )
             for way, (source, target) in enumerate(routes)
         ]
         started.append(batch)
+        return batch, routes
+
+    def publish(index, fields):
+        batch, _ = prepare(index, halo)
         for offset, values in enumerate(fields):
             y_ref[STARTS[index] + offset] = values.reshape(128, 128)
         for way in (4, 5, 6, 7, 2, 3):
@@ -328,18 +322,57 @@
     def layered(parts):
         return jnp.stack([weights[a] * parts[e] for e in range(2) for a in range(8)])
 
+    face_w = const_ref[256:264, :]
+    slopes = jnp.stack([const_ref[264:272, :] + slope[a] for a in range(8)] * 2)
+
+    def materials(elems):
+        mass = layered([face_w * (INV_STEP * elems[2 + e : 3 + e, :]) for e in range(2)])
+        conduct = layered([face_w * elems[e : e + 1, :] for e in range(2)])
+        return mass, conduct, mass + conduct * slopes
+
+    mass, _, diag_local = materials(home_ref[16])
+    home_ref[0:16] = mass * home_ref[0:16]
+    for slot, values in enumerate((home_ref[0:16], mass, diag_local)):
+        y_ref[slot] = values.reshape(128, 128)
+    for slot in range(3):
+        for edge, line in ((0, 0), (1, 7)):
+            face_ref[edge, slot] = y_ref.at[slot][pl.ds(line, 16, stride=8), :]
+    pl.semaphore_wait(barrier, 8 + 8 + 1 + per_run - 1 + 2 * depth - 1)
+
+    batch, routes = prepare(0, entry_halo)
+
+    def launch(way):
+        @pl.when(remote[way])
+        def _():
+            batch[way].start()
+
+        @pl.when(jnp.logical_not(remote[way]))
+        def _():
+            pltpu.make_async_copy(*routes[way], recv_sem.at[0, way]).start()
+
+    for way in (4, 5, 6, 7):
+        launch(way)
+
+    @pl.when(moves)
+    def _():
+        bring.start()
+
+    for way in (2, 3, 0, 1):
+        launch(way)
+
     @pl.when(moves)
     def _():
         bring.wait_recv()
 
-    elems = moved_ref[16]
-    face_w = const_ref[256:264, :]
-    face_slope = const_ref[264:272, :]
-    stiff_w = [face_w * elems[e : e + 1, :] for e in range(2)]
-    mass_w = [face_w * (INV_STEP * elems[2 + e : 3 + e, :]) for e in range(2)]
-    mass = layered(mass_w)
-    conduct = layered(stiff_w)
-    slopes = jnp.stack([face_slope + slope[a] for a in range(8)] * 2)
+    @pl.when(jnp.logical_not(moves))
+    def _():
+        moved_ref[...] = home_ref[...]
+
+    mass, conduct, diag_local = materials(moved_ref[16])
+    mat_ref[0] = mass
+    mat_ref[1] = conduct
+    for slot, values in enumerate((moved_ref[0:16], mass, diag_local)):
+        work_ref[slot] = values.reshape(128, 128)
 
     def stiffness(*fields):
         flats = [values.reshape(128, 128) for values in fields]
@@ -363,10 +396,6 @@
             ).reshape(16, 8, 128)
             for k, values in enumerate(fields)
         ]
-
-    mat_ref[0] = mass
-    mat_ref[1] = conduct
-    publish(0, (mass * moved_ref[0:16], mass, mass + conduct * slopes))
 
     local = lax.broadcasted_iota(jnp.int32, (128, 128), 0) // 8
     hits = []
@@ -395,7 +424,9 @@
                     axis=1,
                 )
             )
-        rows = jnp.concatenate(rows + [jnp.zeros((5, 256), jnp.float32)], axis=0)
+        rows = jnp.concatenate(
+            rows + [jnp.zeros((8 - len(rows), 256), jnp.float32)], axis=0
+        )
         return jnp.dot(rows, hit, precision=HIGH, preferred_element_type=jnp.float32)
 
     depth_copies = [jnp.ones((1, 1), jnp.float32)] * 16
@@ -417,13 +448,13 @@
         return jnp.sum((left * right).reshape(128, 128), axis=0, keepdims=True)
 
     stages = (
-        (tile_a, pos, per_run, layer_peer, layer_steps),
-        (tile_b, spot, 2 * depth, column_peer, column_steps),
+        ((row_b, tile_b), spot, 2 * depth, column_peer, column_steps),
+        ((row_a, tile_a), pos, per_run, layer_peer, layer_steps),
     )
 
     def push(index, stage, tile):
-        ref, slot, _, peer, steps = stages[stage]
-        own = ref.at[index, slot]
+        refs, slot, _, peer, steps = stages[stage]
+        own = refs[index].at[slot]
         own[...] = tile
         for step in steps:
             pltpu.make_async_remote_copy(
@@ -436,8 +467,8 @@
             ).start()
 
     def rest(index, stage):
-        ref, _, count, peer, _ = stages[stage]
-        others = ref.at[index, pl.ds(0, count - 1)]
+        refs, _, count, peer, _ = stages[stage]
+        others = refs[index].at[pl.ds(0, count - 1)]
         return pltpu.make_async_remote_copy(
             src_ref=others,
             dst_ref=others,
@@ -449,9 +480,11 @@
 
     def pull(index, stage):
         rest(index, stage).wait_recv()
-        return jnp.sum(stages[stage][0][index], axis=0)
+        return jnp.sum(stages[stage][0][index][...], axis=0)
 
     weighted = mat_ref[3]
+
+    zeros = jnp.zeros((1, 128), jnp.float32)
 
     def moments(first, second, third, applied):
         m = [dot_rows(weighted * first, first), dot_rows(weighted * first, second)]
@@ -459,14 +492,15 @@
         m.append(dot_rows(weighted * second, third))
         m.append(dot_rows(weighted * third, third))
         m.append(dot_rows(third, applied) - SHIFT * m[4])
-        m = [part + pltpu.roll(part, 64, axis=1) for part in m]
-        return [jnp.where(lane[0:1] < 64, m[2 * k], m[2 * k + 1]) for k in range(3)]
+        m = jnp.concatenate(m + [zeros, zeros], axis=0)
+        for shift in (64, 32, 16):
+            m = m + pltpu.roll(m, shift, axis=1)
+        return jnp.sum(jnp.where(lane // 16 == sub, m, 0.0), axis=0, keepdims=True)
 
     def coefficients(tile):
-        left = jnp.where(lane < 64, tile, 0.0)
-        left_sum = jnp.broadcast_to(jnp.sum(left, axis=1, keepdims=True), (8, 128))
-        right_sum = jnp.broadcast_to(jnp.sum(tile - left, axis=1, keepdims=True), (8, 128))
-        m = [(right_sum if k % 2 else left_sum)[k // 2 : k // 2 + 1] for k in range(6)]
+        m = jnp.where(lane // 16 == sub, tile, 0.0)
+        m = jnp.broadcast_to(jnp.sum(m, axis=1, keepdims=True), (8, 128))
+        m = [m[k : k + 1] for k in range(6)]
         a = [m[k + 1] + SHIFT * m[k] for k in range(5)]
         pivot0 = a[0]
         l1 = a[1] / pivot0
@@ -510,48 +544,41 @@
             for k, values in enumerate(previous)
         ]
 
-    zeros = jnp.zeros((1, 128), jnp.float32)
     v0 = gathered(0) * inv_diag
     publish(1, stiffness(v0))
+    keep(3, mat_ref[4])
     (v1,) = advance(1, (v0,))
     publish(2, stiffness(v1))
     (v2,) = advance(2, (v1,))
     basis = (v0, v1, v2)
     w0 = [values * mat_ref[4] for values in basis]
     publish(3, stiffness(*w0))
-    sums = source_sums(basis, hits[1])
-    push(
-        0,
-        0,
-        jnp.concatenate(
-            moments(v0, v1, v2, stiffness(v2)[0]) + [sums[0:3], zeros, zeros], axis=0
-        ),
-    )
+    push(0, 0, moments(v0, v1, v2, stiffness(v2)[0]))
     w1 = advance(3, w0)
     publish(4, stiffness(*w1))
     push(0, 1, pull(0, 0))
     w2 = advance(4, w1)
     tile = pull(0, 1)
     coef = coefficients(tile)
-    later_grad = blend(coef, [tile[3 + k : 4 + k] for k in range(3)])
     wide_coef = [c[None] for c in coef]
     later = blend(wide_coef, basis)
     basis = [blend(wide_coef, fields) for fields in (w0, w1, w2)]
     sums = source_sums(basis, hits[0])
+    later_sums = source_sums((later,), hits[1])
     push(
         1,
         0,
         jnp.concatenate(
-            moments(*basis, stiffness(basis[2])[0]) + [sums[0:3], zeros, zeros], axis=0
+            [moments(*basis, stiffness(basis[2])[0]), sums[0:3], later_sums[0:1]], axis=0
         ),
     )
     keep(0, later)
-    for k in range(3):
-        keep(1 + k, basis[k])
+    keep(1, basis[1])
+    keep(2, basis[2])
     push(1, 1, pull(1, 0))
     tile = pull(1, 1)
-    coef = coefficients(tile)
-    earlier_grad = blend(coef, [tile[3 + k : 4 + k] for k in range(3)])
+    coef = coefficients(tile[0:1])
+    earlier_grad = blend(coef, [tile[1 + k : 2 + k] for k in range(3)])
 
     @pl.when(moves)
     def _():
@@ -559,14 +586,18 @@
             send_back.wait_recv()
 
     second_ref[...] = back_ref[0]
-    first_ref[...] = blend([c[None] for c in coef], [back_ref[1 + k] for k in range(3)])
+    first_ref[...] = blend(
+        [c[None] for c in coef], (back_ref[0] * back_ref[3], back_ref[1], back_ref[2])
+    )
     scale = 1.0 / (8.0 * INV_STEP)
     grad_ref[0:1, :] = earlier_grad * scale
-    grad_ref[1:2, :] = later_grad * scale
+    grad_ref[1:2, :] = tile[4:5] * scale
     for index in range(2):
         for stage in range(2):
             rest(index, stage).wait_send()
-    for batch in started:
+    for way, copy in enumerate(started[0]):
+        pl.when(remote[way])(copy.wait_send)
+    for batch in started[1:]:
         for copy in batch:
             copy.wait_send()
 
@@ -619,8 +650,10 @@
                 pltpu.VMEM((6, TOTAL, 8, 128), jnp.float32),
                 pltpu.VMEM((TOTAL, 128, 128), jnp.float32),
                 pltpu.VMEM((5, 16, 8, 128), jnp.float32),
-                pltpu.VMEM((2, run, 8, 128), jnp.float32),
-                pltpu.VMEM((2, stack, 8, 128), jnp.float32),
+                pltpu.VMEM((run, 1, 128), jnp.float32),
+                pltpu.VMEM((stack, 1, 128), jnp.float32),
+                pltpu.VMEM((run, 5, 128), jnp.float32),
+                pltpu.VMEM((stack, 5, 128), jnp.float32),
                 pltpu.SemaphoreType.DMA((5, 8)),
                 pltpu.SemaphoreType.DMA((5, 8)),
                 pltpu.SemaphoreType.DMA((2, 2)),

time: 53.1 us -> 49.7 us (0.936)
  Pallas kernels: 52.3 us -> 49 us
    pallas_call x1, Pallas kernels: 51.7 us -> 48.3 us  [per_device(): pl.pallas_call(functools.partial(kernel, shape, weights, slope), out_shap...]
where the time goes in v5:
time: 49.7 us; the launch traced here: 49.6 us
  Pallas kernels  49 us (99%)
  between operations  0.64 us (1%)
    pallas_call x1, Pallas kernels, per_device(): pl.pallas_call(functools.partial(kernel, shape, weights, slope), out_shap...  48.3 us

profile of v5, /device:TPU:1, one launch (start us, length us, event | category | flops | bytes accessed | tf_op | source)
XLA Modules:
  0.0 49.6 jit_solution(14763864954026926278)
XLA Ops:
  0.6 48.3 %shard_map.76 = (f32[16,8,128]{2,1,0:T(8,128)S(1)}, f32[16,8,128]{2,1,0:T(8,128)S(1)}, f32[2,128]{1,0:T(2,128)S(1)}) custom-call(f32[16,8,128]{2,1,0:T(8,128)} %cot_hbm.1, f32[2,1,16]{2,1,0:T(1,128)} %kap_hbm.1, f32[2,1,16]{2,1,0:T(1,128)} %cap_hbm.1, s32[2,128]{1,0:T(2,128)} %src_hbm.1, f32[272,128]{1,0:T(8,128)} %constant.2.clone.const_hbm), custom_call_target="tpu_custom_call" | custom-call | tf_op jit(solution)/shard_map/pallas_call | solution.py:633
  49.0 0.7 %shard_map.77 = (f32[16,8,128]{2,1,0:T(8,128)}, f32[16,8,128]{2,1,0:T(8,128)}, f32[2,128]{1,0:T(2,128)}) custom-call(f32[16,8,128]{2,1,0:T(8,128)S(1)} %get-tuple-element.6.refs_0_, f32[16,8,128]{2,1,0:T(8,128)S(1)} %get-tuple-element.7.refs_1_, f32[2,128]{1,0:T(2,128)S(1)} %get-tuple-element.8.refs_2_), custom_call_target="tpu_custom_call" | custom-call | tf_op jit(solution)/shard_map/pallas_call | solution.py:667

commit v6 on v5

--- a/solution.py
+++ b/solution.py
@@ -89,6 +89,8 @@
     cap_ref,
     src_ref,
     const_ref,
+    cot_ref,
+    elems_ref,
     home_ref,
     moved_ref,
     back_ref,
@@ -117,7 +119,7 @@
             (
                 (kap_hbm, kap_ref),
                 (cap_hbm, cap_ref),
-                (cot_hbm, home_ref.at[pl.ds(0, 16)]),
+                (cot_hbm, cot_ref),
                 (const_hbm, const_ref),
                 (src_hbm, src_ref),
             )
@@ -194,19 +196,14 @@
     entry_halo = tuple(host(*block) for block in around(high, wide))
     remote = [jnp.logical_or(a != high, b != wide) for a, b in entry_halo]
     barrier = pltpu.get_barrier_semaphore()
-    for device in halo + around(h, p) + (source,):
-        pl.semaphore_signal(barrier, inc=1, device_id=device, device_id_type=MESH)
-
-    def greet_layer(step, carry):
-        pl.semaphore_signal(barrier, inc=1, device_id=layer_peer(step), device_id_type=MESH)
-        return carry
-
-    def greet_column(step, carry):
-        pl.semaphore_signal(barrier, inc=1, device_id=column_peer(step), device_id_type=MESH)
-        return carry
-
-    lax.fori_loop(1, per_run, greet_layer, 0)
-    lax.fori_loop(1, 2 * depth, greet_column, 0)
+    def greet(devices):
+        for device in devices:
+            pl.semaphore_signal(barrier, inc=1, device_id=device, device_id_type=MESH)
+
+    greet(around(h, p)[::-1] + (source,))
+    greet(column_peer(step) for step in column_steps)
+    greet(layer_peer(step) for step in layer_steps)
+    greet(halo[::-1])
 
     has_p_lo = jnp.where(p > 0, 1.0, 0.0)
     has_p_hi = jnp.where(p < planes - 1, 1.0, 0.0)
@@ -230,7 +227,7 @@
     for load in loads[:2]:
         load.wait()
     elems = jnp.concatenate([kap_ref[0], kap_ref[1], cap_ref[0], cap_ref[1]] * 2, axis=0)
-    home_ref[16] = jnp.dot(elems, spread, precision=HIGH, preferred_element_type=jnp.float32)
+    elems_ref[...] = jnp.dot(elems, spread, precision=HIGH, preferred_element_type=jnp.float32)
     for load in loads[2:]:
         load.wait()
 
@@ -244,7 +241,10 @@
             device_id_type=MESH,
         )
 
-    bring = move(0, home_ref, moved_ref, target)
+    bring = (
+        move(0, elems_ref, moved_ref, target),
+        move(5, home_ref, work_ref.at[0], target),
+    )
 
     started = []
 
@@ -291,26 +291,29 @@
         for offset, values in enumerate(fields):
             work_ref[STARTS[index] + offset] = values.reshape(128, 128)
 
+    from_low = (row_first * (has_p_lo * has_h_lo), row_last * (has_p_hi * has_h_lo))
+    from_high = (row_first * (has_p_lo * has_h_hi), row_last * (has_p_hi * has_h_hi))
+
     def arrive(index):
-        for copy in started[index]:
+        for copy in started[index][:4]:
+            copy.wait_recv()
+        for slot in range(STARTS[index], STARTS[index] + FIELDS[index]):
+            work = work_ref.at[slot]
+            work[pl.ds(0, 16, stride=8), :] += has_p_lo * plane_in[0, slot]
+            work[pl.ds(7, 16, stride=8), :] += has_p_hi * plane_in[1, slot]
+            work[0:8, :] += has_h_lo * height_in[0, slot]
+            work[120:128, :] += has_h_hi * height_in[1, slot]
+        for copy in started[index][4:]:
             copy.wait_recv()
 
     def gathered(slot):
         work = work_ref.at[slot]
-        work[pl.ds(0, 16, stride=8), :] += has_p_lo * plane_in[0, slot]
-        work[pl.ds(7, 16, stride=8), :] += has_p_hi * plane_in[1, slot]
-        low = (
-            height_in[0, slot]
-            + (row_first * has_p_lo) * pltpu.roll(height_in[2, slot], 1, axis=0)
-            + (row_last * has_p_hi) * pltpu.roll(height_in[3, slot], 7, axis=0)
-        )
-        high = (
-            height_in[1, slot]
-            + (row_first * has_p_lo) * pltpu.roll(height_in[4, slot], 1, axis=0)
-            + (row_last * has_p_hi) * pltpu.roll(height_in[5, slot], 7, axis=0)
-        )
-        work[0:8, :] += has_h_lo * low
-        work[120:128, :] += has_h_hi * high
+        work[0:8, :] += from_low[0] * pltpu.roll(height_in[2, slot], 1, axis=0) + from_low[
+            1
+        ] * pltpu.roll(height_in[3, slot], 7, axis=0)
+        work[120:128, :] += from_high[0] * pltpu.roll(
+            height_in[4, slot], 1, axis=0
+        ) + from_high[1] * pltpu.roll(height_in[5, slot], 7, axis=0)
         joined = work[56:64, :] + work[64:72, :]
         work[56:64, :] = joined
         work[64:72, :] = joined
@@ -330,9 +333,10 @@
         conduct = layered([face_w * elems[e : e + 1, :] for e in range(2)])
         return mass, conduct, mass + conduct * slopes
 
-    mass, _, diag_local = materials(home_ref[16])
-    home_ref[0:16] = mass * home_ref[0:16]
-    for slot, values in enumerate((home_ref[0:16], mass, diag_local)):
+    mass, _, diag_local = materials(elems_ref[...])
+    rhs = mass * cot_ref[...]
+    home_ref[...] = rhs.reshape(128, 128)
+    for slot, values in enumerate((rhs, mass, diag_local)):
         y_ref[slot] = values.reshape(128, 128)
     for slot in range(3):
         for edge, line in ((0, 0), (1, 7)):
@@ -350,29 +354,35 @@
         def _():
             pltpu.make_async_copy(*routes[way], recv_sem.at[0, way]).start()
 
-    for way in (4, 5, 6, 7):
-        launch(way)
-
     @pl.when(moves)
     def _():
-        bring.start()
-
-    for way in (2, 3, 0, 1):
+        bring[0].start()
+
+    for way in (4, 5, 6, 7, 2, 3, 0, 1):
         launch(way)
 
     @pl.when(moves)
     def _():
-        bring.wait_recv()
+        bring[1].start()
+
+    @pl.when(moves)
+    def _():
+        bring[0].wait_recv()
 
     @pl.when(jnp.logical_not(moves))
     def _():
-        moved_ref[...] = home_ref[...]
-
-    mass, conduct, diag_local = materials(moved_ref[16])
+        moved_ref[...] = elems_ref[...]
+        work_ref[0] = home_ref[...]
+
+    mass, conduct, diag_local = materials(moved_ref[...])
     mat_ref[0] = mass
     mat_ref[1] = conduct
-    for slot, values in enumerate((moved_ref[0:16], mass, diag_local)):
-        work_ref[slot] = values.reshape(128, 128)
+    for slot, values in enumerate((mass, diag_local)):
+        work_ref[1 + slot] = values.reshape(128, 128)
+
+    @pl.when(moves)
+    def _():
+        bring[1].wait_recv()
 
     def stiffness(*fields):
         flats = [values.reshape(128, 128) for values in fields]
@@ -411,7 +421,9 @@
             )
         )
 
-    def source_sums(fields, hit):
+    hits = jnp.concatenate(hits, axis=1)
+
+    def source_rows(fields):
         rows = []
         for values in fields:
             weighed = mat_ref[0] * values
@@ -424,10 +436,7 @@
                     axis=1,
                 )
             )
-        rows = jnp.concatenate(
-            rows + [jnp.zeros((8 - len(rows), 256), jnp.float32)], axis=0
-        )
-        return jnp.dot(rows, hit, precision=HIGH, preferred_element_type=jnp.float32)
+        return rows
 
     depth_copies = [jnp.ones((1, 1), jnp.float32)] * 16
     depth_copies[0] = jnp.full((1, 1), 1.0 / (1.0 + has_h_lo))
@@ -441,8 +450,6 @@
     diag = gathered(2)
     inv_diag = 1.0 / diag
     mat_ref[2] = inv_diag
-    mat_ref[3] = jnp.stack([diag[i] * plane_copies * depth_copies[i] for i in range(16)])
-    mat_ref[4] = gathered(1) * inv_diag
 
     def dot_rows(left, right):
         return jnp.sum((left * right).reshape(128, 128), axis=0, keepdims=True)
@@ -481,8 +488,6 @@
     def pull(index, stage):
         rest(index, stage).wait_recv()
         return jnp.sum(stages[stage][0][index][...], axis=0)
-
-    weighted = mat_ref[3]
 
     zeros = jnp.zeros((1, 128), jnp.float32)
 
@@ -546,6 +551,9 @@
 
     v0 = gathered(0) * inv_diag
     publish(1, stiffness(v0))
+    mat_ref[3] = jnp.stack([diag[i] * plane_copies * depth_copies[i] for i in range(16)])
+    weighted = mat_ref[3]
+    mat_ref[4] = gathered(1) * inv_diag
     keep(3, mat_ref[4])
     (v1,) = advance(1, (v0,))
     publish(2, stiffness(v1))
@@ -557,20 +565,25 @@
     w1 = advance(3, w0)
     publish(4, stiffness(*w1))
     push(0, 1, pull(0, 0))
+    rows = source_rows([*basis, *w0, *w1])
     w2 = advance(4, w1)
+    applied = stiffness(*w2)
+    rows = jnp.concatenate(
+        rows + source_rows(w2) + [jnp.zeros((4, 256), jnp.float32)], axis=0
+    )
+    sums = jnp.dot(rows, hits, precision=HIGH, preferred_element_type=jnp.float32)
     tile = pull(0, 1)
     coef = coefficients(tile)
     wide_coef = [c[None] for c in coef]
+    later_sum = blend(coef, [sums[k : k + 1, 128:256] for k in range(3)])
+    earlier_sums = [
+        blend(coef, [sums[3 * n + k : 3 * n + k + 1, 0:128] for k in range(3)]) for n in (1, 2, 3)
+    ]
     later = blend(wide_coef, basis)
     basis = [blend(wide_coef, fields) for fields in (w0, w1, w2)]
-    sums = source_sums(basis, hits[0])
-    later_sums = source_sums((later,), hits[1])
+    applied = blend(wide_coef, applied)
     push(
-        1,
-        0,
-        jnp.concatenate(
-            [moments(*basis, stiffness(basis[2])[0]), sums[0:3], later_sums[0:1]], axis=0
-        ),
+        1, 0, jnp.concatenate([moments(*basis, applied)] + earlier_sums + [later_sum], axis=0)
     )
     keep(0, later)
     keep(1, basis[1])
@@ -603,7 +616,8 @@
 
     @pl.when(moves)
     def _():
-        bring.wait_send()
+        for part in bring:
+            part.wait_send()
         for send_back in returns:
             send_back.wait_send()
 
@@ -640,8 +654,10 @@
                 pltpu.VMEM(capacity.shape, jnp.float32),
                 pltpu.VMEM(sources.shape, jnp.int32),
                 pltpu.VMEM(const.shape, jnp.float32),
-                pltpu.VMEM((17, 8, 128), jnp.float32),
-                pltpu.VMEM((17, 8, 128), jnp.float32),
+                pltpu.VMEM(cotangent.shape, jnp.float32),
+                pltpu.VMEM((8, 128), jnp.float32),
+                pltpu.VMEM((128, 128), jnp.float32),
+                pltpu.VMEM((8, 128), jnp.float32),
                 pltpu.VMEM((4, 16, 8, 128), jnp.float32),
                 pltpu.VMEM((4, 16, 8, 128), jnp.float32),
                 pltpu.VMEM((TOTAL, 128, 128), jnp.float32),
@@ -658,8 +674,8 @@
                 pltpu.SemaphoreType.DMA((5, 8)),
                 pltpu.SemaphoreType.DMA((2, 2)),
                 pltpu.SemaphoreType.DMA((2, 2)),
-                pltpu.SemaphoreType.DMA((5,)),
-                pltpu.SemaphoreType.DMA((5,)),
+                pltpu.SemaphoreType.DMA((6,)),
+                pltpu.SemaphoreType.DMA((6,)),
                 pltpu.SemaphoreType.DMA((5,)),
             ],
             compiler_params=pltpu.CompilerParams(collective_id=0, has_side_effects=True),

time: 49.7 us -> 47.8 us (0.962)
  Pallas kernels: 49 us -> 47.1 us
    pallas_call x1, Pallas kernels: 48.3 us -> 46.4 us  [per_device(): pl.pallas_call(functools.partial(kernel, shape, weights, slope), out_shap...]
where the time goes in v6:
time: 47.8 us; the launch traced here: 47.7 us
  Pallas kernels  47.1 us (99%)
  between operations  0.64 us (1%)
    pallas_call x1, Pallas kernels, per_device(): pl.pallas_call(functools.partial(kernel, shape, weights, slope), out_shap...  46.4 us

profile of v6, /device:TPU:1, one launch (start us, length us, event | category | flops | bytes accessed | tf_op | source)
XLA Modules:
  0.0 47.7 jit_solution(17697377947142099043)
XLA Ops:
  0.6 46.4 %shard_map.76 = (f32[16,8,128]{2,1,0:T(8,128)S(1)}, f32[16,8,128]{2,1,0:T(8,128)S(1)}, f32[2,128]{1,0:T(2,128)S(1)}) custom-call(f32[16,8,128]{2,1,0:T(8,128)} %cot_hbm.1, f32[2,1,16]{2,1,0:T(1,128)} %kap_hbm.1, f32[2,1,16]{2,1,0:T(1,128)} %cap_hbm.1, s32[2,128]{1,0:T(2,128)} %src_hbm.1, f32[272,128]{1,0:T(8,128)} %constant.2.clone.const_hbm), custom_call_target="tpu_custom_call" | custom-call | tf_op jit(solution)/shard_map/pallas_call | solution.py:647
  47.0 0.7 %shard_map.77 = (f32[16,8,128]{2,1,0:T(8,128)}, f32[16,8,128]{2,1,0:T(8,128)}, f32[2,128]{1,0:T(2,128)}) custom-call(f32[16,8,128]{2,1,0:T(8,128)S(1)} %get-tuple-element.6.refs_0_, f32[16,8,128]{2,1,0:T(8,128)S(1)} %get-tuple-element.7.refs_1_, f32[2,128]{1,0:T(2,128)S(1)} %get-tuple-element.8.refs_2_), custom_call_target="tpu_custom_call" | custom-call | tf_op jit(solution)/shard_map/pallas_call | solution.py:683

commit v7 on v6

--- a/solution.py
+++ b/solution.py
@@ -12,8 +12,8 @@
 HIGH = lax.Precision.HIGHEST
 INV_STEP = 20.0
 SHIFT = 0.75
-FIELDS = (3, 1, 1, 3, 3)
-STARTS = (0, 3, 4, 5, 8)
+FIELDS = (2, 2, 1, 3, 3)
+STARTS = (0, 2, 4, 5, 8)
 TOTAL = 11
 
 
@@ -99,6 +99,8 @@
     face_ref,
     plane_in,
     height_in,
+    corner_ref,
+    corner_in,
     work_ref,
     mat_ref,
     row_a,
@@ -203,7 +205,7 @@
     greet(around(h, p)[::-1] + (source,))
     greet(column_peer(step) for step in column_steps)
     greet(layer_peer(step) for step in layer_steps)
-    greet(halo[::-1])
+    greet(halo[4:])
 
     has_p_lo = jnp.where(p > 0, 1.0, 0.0)
     has_p_hi = jnp.where(p < planes - 1, 1.0, 0.0)
@@ -257,10 +259,10 @@
             (face_ref.at[1, slots], plane_in.at[0, slots]),
             (first_rows, height_in.at[1, slots]),
             (last_rows, height_in.at[0, slots]),
-            (first_rows, height_in.at[5, slots]),
-            (first_rows, height_in.at[4, slots]),
-            (last_rows, height_in.at[3, slots]),
-            (last_rows, height_in.at[2, slots]),
+            (corner_ref.at[0, slots], corner_in.at[3, slots]),
+            (corner_ref.at[1, slots], corner_in.at[2, slots]),
+            (corner_ref.at[2, slots], corner_in.at[1, slots]),
+            (corner_ref.at[3, slots], corner_in.at[0, slots]),
         )
         batch = [
             pltpu.make_async_remote_copy(
@@ -276,10 +278,15 @@
         started.append(batch)
         return batch, routes
 
+    def cut_corners(slot):
+        for corner, line in enumerate((0, 7, 120, 127)):
+            corner_ref[corner, slot] = y_ref[slot, line : line + 1]
+
     def publish(index, fields):
         batch, _ = prepare(index, halo)
         for offset, values in enumerate(fields):
             y_ref[STARTS[index] + offset] = values.reshape(128, 128)
+            cut_corners(STARTS[index] + offset)
         for way in (4, 5, 6, 7, 2, 3):
             batch[way].start()
         for offset in range(FIELDS[index]):
@@ -290,6 +297,21 @@
             batch[way].start()
         for offset, values in enumerate(fields):
             work_ref[STARTS[index] + offset] = values.reshape(128, 128)
+        sent(index - 1)
+
+    def sent(index):
+        if index:
+            for copy in started[index]:
+                copy.wait_send()
+            return
+        for way, copy in enumerate(started[0]):
+            pl.when(remote[way])(copy.wait_send)
+
+        @pl.when(moves)
+        def _():
+            for part in bring:
+                part.wait_send()
+
 
     from_low = (row_first * (has_p_lo * has_h_lo), row_last * (has_p_hi * has_h_lo))
     from_high = (row_first * (has_p_lo * has_h_hi), row_last * (has_p_hi * has_h_hi))
@@ -308,12 +330,8 @@
 
     def gathered(slot):
         work = work_ref.at[slot]
-        work[0:8, :] += from_low[0] * pltpu.roll(height_in[2, slot], 1, axis=0) + from_low[
-            1
-        ] * pltpu.roll(height_in[3, slot], 7, axis=0)
-        work[120:128, :] += from_high[0] * pltpu.roll(
-            height_in[4, slot], 1, axis=0
-        ) + from_high[1] * pltpu.roll(height_in[5, slot], 7, axis=0)
+        work[0:8, :] += from_low[0] * corner_in[0, slot] + from_low[1] * corner_in[1, slot]
+        work[120:128, :] += from_high[0] * corner_in[2, slot] + from_high[1] * corner_in[3, slot]
         joined = work[56:64, :] + work[64:72, :]
         work[56:64, :] = joined
         work[64:72, :] = joined
@@ -336,12 +354,13 @@
     mass, _, diag_local = materials(elems_ref[...])
     rhs = mass * cot_ref[...]
     home_ref[...] = rhs.reshape(128, 128)
-    for slot, values in enumerate((rhs, mass, diag_local)):
+    for slot, values in enumerate((rhs, diag_local)):
         y_ref[slot] = values.reshape(128, 128)
-    for slot in range(3):
+        cut_corners(slot)
+    for slot in range(2):
         for edge, line in ((0, 0), (1, 7)):
             face_ref[edge, slot] = y_ref.at[slot][pl.ds(line, 16, stride=8), :]
-    pl.semaphore_wait(barrier, 8 + 8 + 1 + per_run - 1 + 2 * depth - 1)
+    pl.semaphore_wait(barrier, 8 + 4 + 1 + per_run - 1 + 2 * depth - 1)
 
     batch, routes = prepare(0, entry_halo)
 
@@ -377,8 +396,7 @@
     mass, conduct, diag_local = materials(moved_ref[...])
     mat_ref[0] = mass
     mat_ref[1] = conduct
-    for slot, values in enumerate((mass, diag_local)):
-        work_ref[1 + slot] = values.reshape(128, 128)
+    work_ref[1] = diag_local.reshape(128, 128)
 
     @pl.when(moves)
     def _():
@@ -447,7 +465,7 @@
     )
 
     arrive(0)
-    diag = gathered(2)
+    diag = gathered(1)
     inv_diag = 1.0 / diag
     mat_ref[2] = inv_diag
 
@@ -550,13 +568,13 @@
         ]
 
     v0 = gathered(0) * inv_diag
-    publish(1, stiffness(v0))
+    publish(1, (*stiffness(v0), mat_ref[0]))
     mat_ref[3] = jnp.stack([diag[i] * plane_copies * depth_copies[i] for i in range(16)])
     weighted = mat_ref[3]
-    mat_ref[4] = gathered(1) * inv_diag
-    keep(3, mat_ref[4])
     (v1,) = advance(1, (v0,))
     publish(2, stiffness(v1))
+    mat_ref[4] = gathered(STARTS[1] + 1) * mat_ref[2]
+    keep(3, mat_ref[4])
     (v2,) = advance(2, (v1,))
     basis = (v0, v1, v2)
     w0 = [values * mat_ref[4] for values in basis]
@@ -588,38 +606,30 @@
     keep(0, later)
     keep(1, basis[1])
     keep(2, basis[2])
+    sent(4)
+    for stage in range(2):
+        rest(0, stage).wait_send()
     push(1, 1, pull(1, 0))
-    tile = pull(1, 1)
-    coef = coefficients(tile[0:1])
-    earlier_grad = blend(coef, [tile[1 + k : 2 + k] for k in range(3)])
 
     @pl.when(moves)
     def _():
         for send_back in returns:
             send_back.wait_recv()
+            send_back.wait_send()
 
     second_ref[...] = back_ref[0]
+    for stage in range(2):
+        rest(1, stage).wait_send()
+    tile = pull(1, 1)
+    coef = coefficients(tile[0:1])
+    earlier_grad = blend(coef, [tile[1 + k : 2 + k] for k in range(3)])
+
     first_ref[...] = blend(
         [c[None] for c in coef], (back_ref[0] * back_ref[3], back_ref[1], back_ref[2])
     )
     scale = 1.0 / (8.0 * INV_STEP)
     grad_ref[0:1, :] = earlier_grad * scale
     grad_ref[1:2, :] = tile[4:5] * scale
-    for index in range(2):
-        for stage in range(2):
-            rest(index, stage).wait_send()
-    for way, copy in enumerate(started[0]):
-        pl.when(remote[way])(copy.wait_send)
-    for batch in started[1:]:
-        for copy in batch:
-            copy.wait_send()
-
-    @pl.when(moves)
-    def _():
-        for part in bring:
-            part.wait_send()
-        for send_back in returns:
-            send_back.wait_send()
 
 
 def write_out(*refs):
@@ -663,7 +673,9 @@
                 pltpu.VMEM((TOTAL, 128, 128), jnp.float32),
                 pltpu.VMEM((2, TOTAL, 16, 128), jnp.float32),
                 pltpu.VMEM((2, TOTAL, 16, 128), jnp.float32),
-                pltpu.VMEM((6, TOTAL, 8, 128), jnp.float32),
+                pltpu.VMEM((2, TOTAL, 8, 128), jnp.float32),
+                pltpu.VMEM((4, TOTAL, 1, 128), jnp.float32),
+                pltpu.VMEM((4, TOTAL, 1, 128), jnp.float32),
                 pltpu.VMEM((TOTAL, 128, 128), jnp.float32),
                 pltpu.VMEM((5, 16, 8, 128), jnp.float32),
                 pltpu.VMEM((run, 1, 128), jnp.float32),

time: 47.8 us -> 46 us (0.962)
  Pallas kernels: 47.1 us -> 45.2 us
    pallas_call x1, Pallas kernels: 46.4 us -> 44.6 us  [per_device(): pl.pallas_call(functools.partial(kernel, shape, weights, slope), out_shap...]
where the time goes in v7:
time: 46 us; the launch traced here: 45.9 us
  Pallas kernels  45.2 us (98%)
  between operations  0.64 us (1%)
    pallas_call x1, Pallas kernels, per_device(): pl.pallas_call(functools.partial(kernel, shape, weights, slope), out_shap...  44.6 us

profile of v7, /device:TPU:1, one launch (start us, length us, event | category | flops | bytes accessed | tf_op | source)
XLA Modules:
  0.0 45.9 jit_solution(12991045690579442490)
XLA Ops:
  0.6 44.6 %shard_map.76 = (f32[16,8,128]{2,1,0:T(8,128)S(1)}, f32[16,8,128]{2,1,0:T(8,128)S(1)}, f32[2,128]{1,0:T(2,128)S(1)}) custom-call(f32[16,8,128]{2,1,0:T(8,128)} %cot_hbm.1, f32[2,1,16]{2,1,0:T(1,128)} %kap_hbm.1, f32[2,1,16]{2,1,0:T(1,128)} %cap_hbm.1, s32[2,128]{1,0:T(2,128)} %src_hbm.1, f32[272,128]{1,0:T(8,128)} %constant.2.clone.const_hbm), custom_call_target="tpu_custom_call" | custom-call | tf_op jit(solution)/shard_map/pallas_call | solution.py:657
  45.2 0.7 %shard_map.77 = (f32[16,8,128]{2,1,0:T(8,128)}, f32[16,8,128]{2,1,0:T(8,128)}, f32[2,128]{1,0:T(2,128)}) custom-call(f32[16,8,128]{2,1,0:T(8,128)S(1)} %get-tuple-element.6.refs_0_, f32[16,8,128]{2,1,0:T(8,128)S(1)} %get-tuple-element.7.refs_1_, f32[2,128]{1,0:T(2,128)S(1)} %get-tuple-element.8.refs_2_), custom_call_target="tpu_custom_call" | custom-call | tf_op jit(solution)/shard_map/pallas_call | solution.py:695

commit v8 on v7

--- a/solution.py
+++ b/solution.py
@@ -202,8 +202,8 @@
         for device in devices:
             pl.semaphore_signal(barrier, inc=1, device_id=device, device_id_type=MESH)
 
+    greet(column_peer(step) for step in column_steps)
     greet(around(h, p)[::-1] + (source,))
-    greet(column_peer(step) for step in column_steps)
     greet(layer_peer(step) for step in layer_steps)
     greet(halo[4:])
 
@@ -416,6 +416,8 @@
             precision=HIGH,
             preferred_element_type=jnp.float32,
         )
+        if len(fields) > 1:
+            return [stiffness(values)[0] for values in fields]
         return [
             mat_ref[0] * values
             + mat_ref[1]
@@ -574,7 +576,6 @@
     (v1,) = advance(1, (v0,))
     publish(2, stiffness(v1))
     mat_ref[4] = gathered(STARTS[1] + 1) * mat_ref[2]
-    keep(3, mat_ref[4])
     (v2,) = advance(2, (v1,))
     basis = (v0, v1, v2)
     w0 = [values * mat_ref[4] for values in basis]
@@ -583,6 +584,7 @@
     w1 = advance(3, w0)
     publish(4, stiffness(*w1))
     push(0, 1, pull(0, 0))
+    keep(3, mat_ref[4])
     rows = source_rows([*basis, *w0, *w1])
     w2 = advance(4, w1)
     applied = stiffness(*w2)

time: 46 us -> 46.2 us (level)
  no operation moved by 1% of the time
where the time goes in v8:
time: 46.2 us; the launch traced here: 46.1 us
  Pallas kernels  45.4 us (98%)
  between operations  0.64 us (1%)
    pallas_call x1, Pallas kernels, per_device(): pl.pallas_call(functools.partial(kernel, shape, weights, slope), out_shap...  44.7 us

profile of v8, /device:TPU:1, one launch (start us, length us, event | category | flops | bytes accessed | tf_op | source)
XLA Modules:
  0.0 46.1 jit_solution(912719001618717434)
XLA Ops:
  0.6 44.7 %shard_map.76 = (f32[16,8,128]{2,1,0:T(8,128)S(1)}, f32[16,8,128]{2,1,0:T(8,128)S(1)}, f32[2,128]{1,0:T(2,128)S(1)}) custom-call(f32[16,8,128]{2,1,0:T(8,128)} %cot_hbm.1, f32[2,1,16]{2,1,0:T(1,128)} %kap_hbm.1, f32[2,1,16]{2,1,0:T(1,128)} %cap_hbm.1, s32[2,128]{1,0:T(2,128)} %src_hbm.1, f32[272,128]{1,0:T(8,128)} %constant.2.clone.const_hbm), custom_call_target="tpu_custom_call" | custom-call | tf_op jit(solution)/shard_map/pallas_call | solution.py:659
  45.4 0.7 %shard_map.77 = (f32[16,8,128]{2,1,0:T(8,128)}, f32[16,8,128]{2,1,0:T(8,128)}, f32[2,128]{1,0:T(2,128)}) custom-call(f32[16,8,128]{2,1,0:T(8,128)S(1)} %get-tuple-element.6.refs_0_, f32[16,8,128]{2,1,0:T(8,128)S(1)} %get-tuple-element.7.refs_1_, f32[2,128]{1,0:T(2,128)S(1)} %get-tuple-element.8.refs_2_), custom_call_target="tpu_custom_call" | custom-call | tf_op jit(solution)/shard_map/pallas_call | solution.py:697

commit v9 on v7

--- a/solution.py
+++ b/solution.py
@@ -12,8 +12,8 @@
 HIGH = lax.Precision.HIGHEST
 INV_STEP = 20.0
 SHIFT = 0.75
-FIELDS = (2, 2, 1, 3, 3)
-STARTS = (0, 2, 4, 5, 8)
+FIELDS = (2, 1, 1, 3, 3, 1)
+STARTS = (0, 2, 3, 4, 7, 10)
 TOTAL = 11
 
 
@@ -248,7 +248,7 @@
         move(5, home_ref, work_ref.at[0], target),
     )
 
-    started = []
+    started = {}
 
     def prepare(index, devices):
         slots = pl.ds(STARTS[index], FIELDS[index])
@@ -275,7 +275,7 @@
             )
             for way, (source, target) in enumerate(routes)
         ]
-        started.append(batch)
+        started[index] = batch
         return batch, routes
 
     def cut_corners(slot):
@@ -297,7 +297,8 @@
             batch[way].start()
         for offset, values in enumerate(fields):
             work_ref[STARTS[index] + offset] = values.reshape(128, 128)
-        sent(index - 1)
+        if index < 5:
+            sent(index - 1)
 
     def sent(index):
         if index:
@@ -568,12 +569,14 @@
         ]
 
     v0 = gathered(0) * inv_diag
-    publish(1, (*stiffness(v0), mat_ref[0]))
+    publish(1, stiffness(v0))
+    publish(5, (mat_ref[0],))
     mat_ref[3] = jnp.stack([diag[i] * plane_copies * depth_copies[i] for i in range(16)])
     weighted = mat_ref[3]
     (v1,) = advance(1, (v0,))
     publish(2, stiffness(v1))
-    mat_ref[4] = gathered(STARTS[1] + 1) * mat_ref[2]
+    arrive(5)
+    mat_ref[4] = gathered(STARTS[5]) * mat_ref[2]
     keep(3, mat_ref[4])
     (v2,) = advance(2, (v1,))
     basis = (v0, v1, v2)
@@ -607,6 +610,7 @@
     keep(1, basis[1])
     keep(2, basis[2])
     sent(4)
+    sent(5)
     for stage in range(2):
         rest(0, stage).wait_send()
     push(1, 1, pull(1, 0))
@@ -682,8 +686,8 @@
                 pltpu.VMEM((stack, 1, 128), jnp.float32),
                 pltpu.VMEM((run, 5, 128), jnp.float32),
                 pltpu.VMEM((stack, 5, 128), jnp.float32),
-                pltpu.SemaphoreType.DMA((5, 8)),
-                pltpu.SemaphoreType.DMA((5, 8)),
+                pltpu.SemaphoreType.DMA((6, 8)),
+                pltpu.SemaphoreType.DMA((6, 8)),
                 pltpu.SemaphoreType.DMA((2, 2)),
                 pltpu.SemaphoreType.DMA((2, 2)),
                 pltpu.SemaphoreType.DMA((6,)),

time: 46 us -> 46.1 us (level)
  no operation moved by 1% of the time
where the time goes in v9:
time: 46.1 us; the launch traced here: 46 us
  Pallas kernels  45.4 us (98%)
  between operations  0.64 us (1%)
    pallas_call x1, Pallas kernels, per_device(): pl.pallas_call(functools.partial(kernel, shape, weights, slope), out_shap...  44.7 us

profile of v9, /device:TPU:1, one launch (start us, length us, event | category | flops | bytes accessed | tf_op | source)
XLA Modules:
  0.0 46.0 jit_solution(5383038619598000037)
XLA Ops:
  0.6 44.7 %shard_map.76 = (f32[16,8,128]{2,1,0:T(8,128)S(1)}, f32[16,8,128]{2,1,0:T(8,128)S(1)}, f32[2,128]{1,0:T(2,128)S(1)}) custom-call(f32[16,8,128]{2,1,0:T(8,128)} %cot_hbm.1, f32[2,1,16]{2,1,0:T(1,128)} %kap_hbm.1, f32[2,1,16]{2,1,0:T(1,128)} %cap_hbm.1, s32[2,128]{1,0:T(2,128)} %src_hbm.1, f32[272,128]{1,0:T(8,128)} %constant.2.clone.const_hbm), custom_call_target="tpu_custom_call" | custom-call | tf_op jit(solution)/shard_map/pallas_call | solution.py:661
  45.3 0.7 %shard_map.77 = (f32[16,8,128]{2,1,0:T(8,128)}, f32[16,8,128]{2,1,0:T(8,128)}, f32[2,128]{1,0:T(2,128)}) custom-call(f32[16,8,128]{2,1,0:T(8,128)S(1)} %get-tuple-element.6.refs_0_, f32[16,8,128]{2,1,0:T(8,128)S(1)} %get-tuple-element.7.refs_1_, f32[2,128]{1,0:T(2,128)S(1)} %get-tuple-element.8.refs_2_), custom_call_target="tpu_custom_call" | custom-call | tf_op jit(solution)/shard_map/pallas_call | solution.py:699
